TPU v7x, 512 devices: a whole 4x4x16 slice. The times are simulated.
512 devices in a mesh: loc: 512 (over x, y, z, core).
Axes of the slice: x: 4, y: 4, z: 16, core: 2. Of those that a mesh axis runs over, the one named last changes fastest.
Arguments:
- points: float32 [3, 524288], P(None, 'loc'), may hold values from -1 to 1, as said below
- right_sides: float32 [16, 524288], P(None, 'loc')
- skeleton: int32 [8, 131072], P(None, 'loc'), may hold values from 0 to 1023, as said below
- lengthscale: float32 [1], replicated, may hold values from 0.026516505 to 0.06629126
- far_length: float32 [1], replicated, may hold values from 0.4 to 1
- signal: float32 [1], replicated, may hold values from 0.00024414062 to 0.0009765625
- noise_var: float32 [1], replicated, may hold values from 0.5 to 2
Outputs:
- solution: float32 [16, 524288], P(None, 'loc')
- residual: float32 [16, 524288], P(None, 'loc')
- slope_image: float32 [16, 524288], P(None, 'loc')
- trace_terms: float32 [16], replicated
Inputs may be any that keep to these rules, and one draw needn't show every extreme that they name: `points`: unit vectors. `skeleton`: each leaf's 256 entries of a level rise, the j-th in the range j*1024/256 to (j+1)*1024/256 - 1.
All inputs are finite; a program needn't handle non-finite values.
Results may differ from a plain program's by a relative error of at most 0.002.
Values may be sent and summed in bfloat16 or wider, within the bound.
A program may use at most 64 MiB of HBM per device.

v0:
```python
import jax
import jax.numpy as jnp
from jax import lax
from jax.sharding import PartitionSpec as P

ITERS = 2


root_three = 1.7320508075688772
tile_rows = 512


def extended(shard, sides, width):
    for axis, dim in sides:
        count, length = (lax.axis_size(axis), shard.shape[dim])
        up = [(i, (i + 1) % count) for i in range(count - 1)]
        down = [(j, i) for i, j in up]
        last = lax.slice_in_dim(shard, length - width, length, axis=dim)
        leading = lax.slice_in_dim(shard, 0, width, axis=dim)
        before = lax.ppermute(last, axis, up)
        after = lax.ppermute(leading, axis, down)
        shard = jnp.concatenate([before, shard, after], axis=dim)
    return shard


def partner(value, axis, bit):
    mask = 2**bit
    pairs = [(source, source ^ mask) for source in range(lax.axis_size(axis))]
    return lax.ppermute(value, axis, pairs)


def kernel_pair(row_pts, col_pts, length):
    diff_a = row_pts[0][:, None] - col_pts[0][None, :]
    diff_b = row_pts[1][:, None] - col_pts[1][None, :]
    diff_c = row_pts[2][:, None] - col_pts[2][None, :]
    radius = jnp.sqrt(diff_a * diff_a + diff_b * diff_b + diff_c * diff_c)
    scaled = root_three * radius / length
    decay = jnp.exp(-scaled)
    return ((1.0 + scaled) * decay, scaled * scaled * decay)


def contract_rows(vectors, matrix):
    return lax.dot_general(
        vectors, matrix, (((1,), (1,)), ((), ())), preferred_element_type=jnp.float32
    )


def make_block(row_pts, col_pts, length, fwd_vecs):
    row_count = row_pts.shape[1]
    tile_size = min(tile_rows, row_count)
    tile_count = row_count // tile_size
    tile_pts_all = row_pts.reshape(3, tile_count, tile_size).transpose(1, 0, 2)
    back_init = jnp.zeros((1, 1), jnp.float32)

    def one_tile(back_sum, inputs):
        tile_pts, back_tile = inputs
        kernel_vals, slope_vals = kernel_pair(tile_pts, col_pts, length)
        slope_half = slope_vals.astype(jnp.bfloat16)
        forward = contract_rows(fwd_vecs, slope_half)
        return (back_sum, (kernel_vals.astype(jnp.bfloat16), forward))

    backward, outputs = lax.scan(one_tile, back_init, (tile_pts_all, tile_pts_all))
    kernel_block = outputs[0].reshape(row_count, col_pts.shape[1])
    forward = outputs[1].transpose(1, 0, 2).reshape(fwd_vecs.shape[0], row_count)
    return (kernel_block, forward, backward)


def shards(points, right_sides, skeleton, lengthscale, far_length, signal, noise_var):
    length = lengthscale[0]
    far_len = far_length[0]
    signal_var = signal[0]
    nugget = noise_var[0]
    probe_count, row_count = right_sides.shape
    level_count = skeleton.shape[0]
    rank_size = skeleton.shape[1]
    point_total = row_count * lax.axis_size("loc")
    far_scale = 1.0 / (rank_size * rank_size * level_count)
    wide_pts = extended(points, (("loc", 1),), row_count)
    near_cols = [wide_pts[:, :row_count], points, wide_pts[:, 2 * row_count :]]
    own_skel = [jnp.take(points, skeleton[level_id], axis=1) for level_id in range(level_count)]
    couplings = []
    for level_id in range(level_count):
        partner_skel = partner(own_skel[level_id], "loc", level_id + 1)
        couplings.append(kernel_pair(partner_skel, own_skel[level_id], far_len)[0])

    def side_vectors(vec_half):
        widened = extended(vec_half, (("loc", 1),), row_count)
        return [widened[:, :row_count], vec_half, widened[:, 2 * row_count :]]

    def far_part(vec_half, bases):
        result = jnp.zeros(vec_half.shape, jnp.float32)
        for level_id in range(level_count):
            coefs_own = contract_rows(vec_half, bases[level_id])
            remote_coefs = partner(coefs_own, "loc", level_id + 1)
            mixed_half = jnp.dot(
                remote_coefs, couplings[level_id], precision=lax.Precision.HIGHEST
            ).astype(jnp.bfloat16)
            result = result + jnp.dot(
                mixed_half, bases[level_id], preferred_element_type=jnp.float32
            )
        return far_scale * result

    bases = [
        kernel_pair(own_skel[level_id], points, far_len)[0].astype(jnp.bfloat16)
        for level_id in range(level_count)
    ]
    vec_half = jnp.concatenate([right_sides, jnp.ones((1, row_count), jnp.float32)], axis=0).astype(
        jnp.bfloat16
    )
    side_list = side_vectors(vec_half)
    blocks = []
    kernel_part = far_part(vec_half, bases)
    slope_sum = jnp.zeros((probe_count, row_count), jnp.float32)
    for col_id in range(3):
        kernel_block, forward, backward = make_block(
            points, near_cols[col_id], length, side_list[col_id][:probe_count]
        )
        blocks.append(kernel_block)
        kernel_part = kernel_part + contract_rows(side_list[col_id], kernel_block)
        slope_sum = slope_sum + forward
    row_sums = kernel_part[probe_count:]
    slope_image = signal_var * slope_sum
    first_image = nugget * right_sides + signal_var * (
        kernel_part[:probe_count] + row_sums * right_sides
    )
    solution = jnp.zeros_like(right_sides)
    residual = right_sides

    def norms_of(values):
        return lax.psum(jnp.sum(values * values, axis=1), "loc")

    direction = right_sides
    image = first_image
    norm_now = norms_of(residual)
    for sweep in range(ITERS):
        if sweep > 0:
            half_now = direction.astype(jnp.bfloat16)
            sides_now = side_vectors(half_now)
            kernel_now = far_part(half_now, bases)
            for operate_col_id in range(len(blocks)):
                kernel_now = kernel_now + contract_rows(
                    sides_now[operate_col_id], blocks[operate_col_id]
                )
            image = nugget * direction + signal_var * (kernel_now + row_sums * direction)
        alpha = norm_now / lax.psum(jnp.sum(direction * image, axis=1), "loc")
        solution = solution + alpha[:, None] * direction
        residual = residual - alpha[:, None] * image
        if sweep + 1 < ITERS:
            norm_next = norms_of(residual)
            direction = residual + (norm_next / norm_now)[:, None] * direction
            norm_now = norm_next
    trace_terms = lax.psum(jnp.sum(solution * slope_image, axis=1), "loc") / point_total
    return (solution, residual, slope_image, trace_terms)


def solution(mesh):
    placed = (P(None, "loc"), P(None, "loc"), P(None, "loc"), P(), P(), P(), P())
    return jax.shard_map(
        shards,
        mesh=mesh,
        in_specs=placed,
        out_specs=(P(None, "loc"), P(None, "loc"), P(None, "loc"), P()),
        check_vma=False,
    )
```

profile of v0, /device:TPU:1, one launch (start us, length us, event | category | flops | bytes accessed | tf_op | source)
XLA Modules:
  0.0 705.7 jit_solution(17817297203707529565)
XLA Ops:
  0.6 8.7 %collective-permute-start.19 = (f32[3,1024]{1,0:T(4,128)}, f32[3,1024]{1,0:T(4,128)S(1)}, u32[]{:S(2)}, u32[]{:S(2)}) collective-permute-start(f32[3,1024]{1,0:T(4,128)} %param.15), channel_id=1, source_target_pairs={{1,0},{2,1},{3,2},{4,3},{5,4},{6,5},{7,6},{8,7},{9,8},{10,9},{11,1... | collective-permute-start | bytes 36872 | tf_op jit(solution)/shard_map/ppermute | solution.py:21
  12.8 2.4 collective-permute-start.18
  15.2 3.2 collective-permute-start.16
  24.7 9.3 %while.37 = (s32[]{:T(128)}, bf16[2,512,1024]{2,1,0:T(8,128)(2,1)S(1)}, f32[2,16,512]{2,1,0:T(8,128)S(1)}, f32[2,3,512]{2,1,0:T(4,128)S(1)}, f32[3,1024]{1,0:T(4...) while((s32[]{:T(128)}, ...), condition=%wide.region_5.7_spmd, body=%wide.region_4.6_spmd.sunk | while | flops 31457284 | bytes 1188009 | solution.py:62
  24.8 2.2 fusion.187
  27.0 2.3 fusion.188
  29.3 2.2 fusion.187
  31.5 2.3 fusion.188
  47.9 2.4 gather_fusion.7
  65.9 5.1 collective-permute-start.3
  71.4 6.5 collective-permute-done.3
  77.9 6.0 collective-permute-start.5
  84.2 11.8 %collective-permute-done.5 = f32[3,256]{0,1:T(8,128)S(1)} collective-permute-done((f32[3,256]{0,1:T(8,128)S(1)}, f32[3,256]{0,1:T(8,128)S(1)}, u32[]{:S(2)}, u32[]{:S(2)}) %collective-permute-start.5) | collective-permute-done | bytes 3104 | tf_op jit(solution)/shard_map/ppermute | solution.py:29
  96.0 11.3 %collective-permute-start.7 = (f32[3,256]{0,1:T(8,128)S(1)}, f32[3,256]{0,1:T(8,128)S(1)}, u32[]{:S(2)}, u32[]{:S(2)}) collective-permute-start(f32[3,256]{0,1:T(8,128)S(1)} %select_bitcast_fusion.4), channel_id=1, source_target_pairs={{0,16},{1,17},{2,18},{3,19},{4,20},{5,21},{6,22},{7,23},{8,24},{9,... | collective-permute-start | bytes 9224 | tf_op jit(solution)/shard_map/ppermute | solution.py:29
  107.6 5.2 collective-permute-done.7
  112.8 4.0 collective-permute-start.9
  119.2 5.0 collective-permute-start.11
  124.4 2.2 collective-permute-done.11
  126.6 3.1 collective-permute-start.13
  130.0 2.3 collective-permute-done.13
  132.3 11.5 %collective-permute-start.15 = (f32[3,256]{0,1:T(8,128)S(1)}, f32[3,256]{0,1:T(8,128)S(1)}, u32[]{:S(2)}, u32[]{:S(2)}) collective-permute-start(f32[3,256]{0,1:T(8,128)S(1)} %select_bitcast_fusion), channel_id=1, source_target_pairs={{0,256},{1,257},{2,258},{3,259},{4,260},{5,261},{6,262},{7,263},{8... | collective-permute-start | bytes 9224 | tf_op jit(solution)/shard_map/ppermute | solution.py:29
  148.0 2.5 collective-permute-done
  156.1 5.1 collective-permute-start.4
  164.8 7.0 collective-permute-start.6
  173.3 4.7 collective-permute-done.6
  178.0 2.7 collective-permute-start.8
  182.6 5.3 collective-permute-start.10
  189.4 2.4 collective-permute-start.12
  194.0 5.3 collective-permute-start.14
  203.2 9.1 %while.38 = (s32[]{:T(128)}, bf16[2,512,1024]{2,1,0:T(8,128)(2,1)S(1)}, f32[2,16,512]{2,1,0:T(8,128)S(1)}, f32[2,3,512]{2,1,0:T(4,128)S(1)}, f32[3,1024]{1,0:T(4...) while((s32[]{:T(128)}, ...), condition=%wide.region_7.9_spmd, body=%wide.region_6.8_spmd.sunk | while | flops 31457284 | bytes 1188009 | solution.py:62
  203.2 2.2 fusion.191
  205.4 2.3 fusion.192
  210.0 2.3 fusion.192
  213.9 9.1 %while.36 = (s32[]{:T(128)}, bf16[2,512,1024]{2,1,0:T(8,128)(2,1)S(1)}, f32[2,16,512]{2,1,0:T(8,128)S(1)}, f32[2,3,512]{2,1,0:T(4,128)S(1)}, f32[3,1024]{1,0:T(4...) while((s32[]{:T(128)}, ...), condition=%wide.region_3.5_spmd, body=%wide.region_2.4_spmd.sunk | while | flops 31457284 | bytes 1188009 | solution.py:62
  216.1 2.3 fusion.184
  218.5 2.2 fusion.183
  220.7 2.3 fusion.184
  226.2 113.3 %all-reduce.1 = (f32[16]{0:T(128)S(1)}, f32[16]{0:T(128)S(1)}) all-reduce(f32[16]{0:T(128)S(1)} %get-tuple-element.174, f32[16]{0:T(128)S(1)} %get-tuple-element.173), channel_id=1, replica_groups=mesh['loc'=512] {'loc'}, use_global_device_ids=true, to_apply=%region_1.2 | all-reduce | flops 32 | bytes 256 | tf_op jit(solution)/shard_map/psum | solution.py:130
  339.7 100.4 %psum.37 = f32[16]{0:T(128)S(1)} all-reduce(f32[16]{0:T(128)S(1)} %multiply_reduce_fusion.2), channel_id=1, replica_groups=mesh['loc'=512] {'loc'}, use_global_device_ids=true, to_apply=%region_11.13 | all-reduce | flops 16 | bytes 128 | tf_op jit(solution)/shard_map/psum | solution.py:130
  440.2 2.2 fusion.114
  442.4 3.4 collective-permute-start.28
  451.8 3.5 collective-permute-start.21
  460.9 4.3 collective-permute-start.22
  465.3 8.4 %collective-permute-start.23 = (f32[16,256]{1,0:T(8,128)S(1)}, f32[16,256]{1,0:T(8,128)S(1)}, u32[]{:S(2)}, u32[]{:S(2)}) collective-permute-start(f32[16,256]{1,0:T(8,128)S(1)} %fusion.100), channel_id=1, source_target_pairs={{0,16},{1,17},{2,18},{3,19},{4,20},{5,21},{6,22},{7,23},{8,24},{9,... | collective-permute-start | bytes 49160 | tf_op jit(solution)/shard_map/ppermute | solution.py:29
  478.5 5.5 collective-permute-start.25
  489.1 4.3 collective-permute-start.27
  501.4 104.3 %psum.38 = f32[16]{0:T(128)S(1)} all-reduce(f32[16]{0:T(128)S(1)} %get-tuple-element.253), channel_id=1, replica_groups=mesh['loc'=512] {'loc'}, use_global_device_ids=true, to_apply=%region_13.15 | all-reduce | flops 16 | bytes 128 | tf_op jit(solution)/shard_map/psum | solution.py:145
  606.5 98.2 %psum.39 = f32[16]{0:T(128)S(1)} all-reduce(f32[16]{0:T(128)S(1)} %get-tuple-element.219), channel_id=1, replica_groups=mesh['loc'=512] {'loc'}, use_global_device_ids=true, to_apply=%region_15.17 | all-reduce | flops 16 | bytes 128 | tf_op jit(solution)/shard_map/psum | solution.py:152
  (309 shorter events, 104.3 us)
Async XLA Ops:
  0.6 24.1 %copy-start.4 = (f32[3,1024]{1,0:T(4,128)S(1)}, f32[3,1024]{1,0:T(4,128)}, u32[]{:S(2)}) copy-start(f32[3,1024]{1,0:T(4,128)} %param.15) | copy-start | bytes 36868
  0.6 202.3 %collective-permute-start.19 = (f32[3,1024]{1,0:T(4,128)}, f32[3,1024]{1,0:T(4,128)S(1)}, u32[]{:S(2)}, u32[]{:S(2)}) collective-permute-start(f32[3,1024]{1,0:T(4,128)} %param.15), channel_id=1, source_target_pairs={{1,0},{2,1},{3,2},{4,3},{5,4},{6,5},{7,6},{8,7},{9,8},{10,9},{11,1... | collective-permute-start | bytes 36872 | tf_op jit(solution)/shard_map/ppermute | solution.py:21
  9.4 204.2 %collective-permute-start.17 = (f32[3,1024]{1,0:T(4,128)}, f32[3,1024]{1,0:T(4,128)S(1)}, u32[]{:S(2)}, u32[]{:S(2)}) collective-permute-start(f32[3,1024]{1,0:T(4,128)} %param.15), channel_id=1, source_target_pairs={{0,1},{1,2},{2,3},{3,4},{4,5},{5,6},{6,7},{7,8},{8,9},{9,10},{10,1... | collective-permute-start | bytes 36872 | tf_op jit(solution)/shard_map/ppermute | solution.py:20
  12.8 189.3 %collective-permute-start.18 = (bf16[17,1024]{1,0:T(8,128)(2,1)}, bf16[17,1024]{1,0:T(8,128)(2,1)}, u32[]{:S(2)}, u32[]{:S(2)}) collective-permute-start(bf16[17,1024]{1,0:T(8,128)(2,1)} %concatenate.3), channel_id=1, source_target_pairs={{1,0},{2,1},{3,2},{4,3},{5,4},{6,5},{7,6},{8,7},{9,8},{10,9},{11,1... | collective-permute-start | bytes 104456 | tf_op jit(solution)/shard_map/ppermute | solution.py:21
  15.2 197.1 %collective-permute-start.16 = (bf16[17,1024]{1,0:T(8,128)(2,1)}, bf16[17,1024]{1,0:T(8,128)(2,1)}, u32[]{:S(2)}, u32[]{:S(2)}) collective-permute-start(bf16[17,1024]{1,0:T(8,128)(2,1)} %concatenate.3), channel_id=1, source_target_pairs={{0,1},{1,2},{2,3},{3,4},{4,5},{5,6},{6,7},{7,8},{8,9},{9,10},{10,1... | collective-permute-start | bytes 104456 | tf_op jit(solution)/shard_map/ppermute | solution.py:20
  21.2 44.7 %collective-permute-start.1 = (f32[3,256]{0,1:T(8,128)S(1)}, f32[3,256]{0,1:T(8,128)S(1)}, u32[]{:S(2)}, u32[]{:S(2)}) collective-permute-start(f32[3,256]{0,1:T(8,128)S(1)} %select_bitcast_fusion.7), channel_id=1, source_target_pairs={{0,2},{1,3},{2,0},{3,1},{4,6},{5,7},{6,4},{7,5},{8,10},{9,11},{10,... | collective-permute-start | bytes 9224 | tf_op jit(solution)/shard_map/ppermute | solution.py:29
  34.1 29.9 %copy-start.3 = (bf16[2,512,1024]{2,1,0:T(8,128)(2,1)}, bf16[2,512,1024]{2,1,0:T(8,128)(2,1)S(1)}, u32[]{:S(2)}) copy-start(bf16[2,512,1024]{2,1,0:T(8,128)(2,1)S(1)} %get-tuple-element.120) | copy-start | bytes 6291460
  36.9 16.2 %copy-start.40 = (f32[256]{0:T(256)}, f32[256]{0:T(256)S(1)}, u32[]{:S(2)}) copy-start(f32[256]{0:T(256)S(1)} %get-tuple-element.164) | copy-start | bytes 3076
  36.9 16.2 %copy-start.42 = (f32[256]{0:T(256)}, f32[256]{0:T(256)S(1)}, u32[]{:S(2)}) copy-start(f32[256]{0:T(256)S(1)} %get-tuple-element.165) | copy-start | bytes 3076
  36.9 16.2 %copy-start.44 = (f32[256]{0:T(256)}, f32[256]{0:T(256)S(1)}, u32[]{:S(2)}) copy-start(f32[256]{0:T(256)S(1)} %get-tuple-element.166) | copy-start | bytes 3076
  39.1 15.6 %copy-start.34 = (f32[256]{0:T(256)}, f32[256]{0:T(256)S(1)}, u32[]{:S(2)}) copy-start(f32[256]{0:T(256)S(1)} %get-tuple-element.158) | copy-start | bytes 3076
  39.1 15.6 %copy-start.36 = (f32[256]{0:T(256)}, f32[256]{0:T(256)S(1)}, u32[]{:S(2)}) copy-start(f32[256]{0:T(256)S(1)} %get-tuple-element.159) | copy-start | bytes 3076
  39.1 15.5 %copy-start.38 = (f32[256]{0:T(256)}, f32[256]{0:T(256)S(1)}, u32[]{:S(2)}) copy-start(f32[256]{0:T(256)S(1)} %get-tuple-element.160) | copy-start | bytes 3076
  41.3 14.9 %copy-start.28 = (f32[256]{0:T(256)}, f32[256]{0:T(256)S(1)}, u32[]{:S(2)}) copy-start(f32[256]{0:T(256)S(1)} %get-tuple-element.152) | copy-start | bytes 3076
  64.6 81.2 %copy-start.65 = (f32[17,256]{1,0:T(8,128)S(1)}, f32[17,256]{1,0:T(8,128)}, u32[]{:S(2)}) copy-start(f32[17,256]{1,0:T(8,128)} %fusion.55) | copy-start | bytes 52228
  64.6 85.9 %copy-start.64 = (f32[17,256]{1,0:T(8,128)S(1)}, f32[17,256]{1,0:T(8,128)}, u32[]{:S(2)}) copy-start(f32[17,256]{1,0:T(8,128)} %fusion.53) | copy-start | bytes 52228
  65.9 12.0 %collective-permute-start.3 = (f32[3,256]{0,1:T(8,128)S(1)}, f32[3,256]{0,1:T(8,128)S(1)}, u32[]{:S(2)}, u32[]{:S(2)}) collective-permute-start(f32[3,256]{0,1:T(8,128)S(1)} %select_bitcast_fusion.6), channel_id=1, source_target_pairs={{0,4},{1,5},{2,6},{3,7},{4,0},{5,1},{6,2},{7,3},{8,12},{9,13},{10,... | collective-permute-start | bytes 9224 | tf_op jit(solution)/shard_map/ppermute | solution.py:29
  71.3 81.6 %copy-start.52 = (f32[256]{0:T(256)}, f32[256]{0:T(256)S(1)}, u32[]{:S(2)}) copy-start(f32[256]{0:T(256)S(1)} %get-tuple-element.167) | copy-start | bytes 3076
  71.3 81.6 %copy-start.54 = (f32[256]{0:T(256)}, f32[256]{0:T(256)S(1)}, u32[]{:S(2)}) copy-start(f32[256]{0:T(256)S(1)} %get-tuple-element.168) | copy-start | bytes 3076
  71.3 81.6 %copy-start.56 = (f32[256]{0:T(256)}, f32[256]{0:T(256)S(1)}, u32[]{:S(2)}) copy-start(f32[256]{0:T(256)S(1)} %get-tuple-element.169) | copy-start | bytes 3076
  77.9 18.1 %collective-permute-start.5 = (f32[3,256]{0,1:T(8,128)S(1)}, f32[3,256]{0,1:T(8,128)S(1)}, u32[]{:S(2)}, u32[]{:S(2)}) collective-permute-start(f32[3,256]{0,1:T(8,128)S(1)} %select_bitcast_fusion.5), channel_id=1, source_target_pairs={{0,8},{1,9},{2,10},{3,11},{4,12},{5,13},{6,14},{7,15},{8,0},{9,1},... | collective-permute-start | bytes 9224 | tf_op jit(solution)/shard_map/ppermute | solution.py:29
  84.2 77.0 %copy-start.46 = (f32[256]{0:T(256)}, f32[256]{0:T(256)S(1)}, u32[]{:S(2)}) copy-start(f32[256]{0:T(256)S(1)} %get-tuple-element.161) | copy-start | bytes 3076
  84.2 77.0 %copy-start.48 = (f32[256]{0:T(256)}, f32[256]{0:T(256)S(1)}, u32[]{:S(2)}) copy-start(f32[256]{0:T(256)S(1)} %get-tuple-element.162) | copy-start | bytes 3076
  84.2 77.0 %copy-start.50 = (f32[256]{0:T(256)}, f32[256]{0:T(256)S(1)}, u32[]{:S(2)}) copy-start(f32[256]{0:T(256)S(1)} %get-tuple-element.163) | copy-start | bytes 3076
  96.0 16.8 %collective-permute-start.7 = (f32[3,256]{0,1:T(8,128)S(1)}, f32[3,256]{0,1:T(8,128)S(1)}, u32[]{:S(2)}, u32[]{:S(2)}) collective-permute-start(f32[3,256]{0,1:T(8,128)S(1)} %select_bitcast_fusion.4), channel_id=1, source_target_pairs={{0,16},{1,17},{2,18},{3,19},{4,20},{5,21},{6,22},{7,23},{8,24},{9,... | collective-permute-start | bytes 9224 | tf_op jit(solution)/shard_map/ppermute | solution.py:29
  112.8 6.4 collective-permute-start.9
  119.2 7.5 %collective-permute-start.11 = (f32[3,256]{0,1:T(8,128)S(1)}, f32[3,256]{0,1:T(8,128)S(1)}, u32[]{:S(2)}, u32[]{:S(2)}) collective-permute-start(f32[3,256]{0,1:T(8,128)S(1)} %select_bitcast_fusion.2), channel_id=1, source_target_pairs={{0,64},{1,65},{2,66},{3,67},{4,68},{5,69},{6,70},{7,71},{8,72},{9,... | collective-permute-start | bytes 9224 | tf_op jit(solution)/shard_map/ppermute | solution.py:29
  126.6 5.7 collective-permute-start.13
  132.3 13.4 %collective-permute-start.15 = (f32[3,256]{0,1:T(8,128)S(1)}, f32[3,256]{0,1:T(8,128)S(1)}, u32[]{:S(2)}, u32[]{:S(2)}) collective-permute-start(f32[3,256]{0,1:T(8,128)S(1)} %select_bitcast_fusion), channel_id=1, source_target_pairs={{0,256},{1,257},{2,258},{3,259},{4,260},{5,261},{6,262},{7,263},{8... | collective-permute-start | bytes 9224 | tf_op jit(solution)/shard_map/ppermute | solution.py:29
  145.8 4.7 collective-permute-start
  150.5 5.6 collective-permute-start.2
  156.1 8.7 %collective-permute-start.4 = (f32[17,256]{1,0:T(8,128)S(1)}, f32[17,256]{1,0:T(8,128)S(1)}, u32[]{:S(2)}, u32[]{:S(2)}) collective-permute-start(f32[17,256]{1,0:T(8,128)S(1)} %copy-done.63), channel_id=1, source_target_pairs={{0,8},{1,9},{2,10},{3,11},{4,12},{5,13},{6,14},{7,15},{8,0},{9,1},... | collective-permute-start | bytes 52232 | tf_op jit(solution)/shard_map/ppermute | solution.py:29
  164.8 13.3 %collective-permute-start.6 = (f32[17,256]{1,0:T(8,128)S(1)}, f32[17,256]{1,0:T(8,128)S(1)}, u32[]{:S(2)}, u32[]{:S(2)}) collective-permute-start(f32[17,256]{1,0:T(8,128)S(1)} %copy-done.62), channel_id=1, source_target_pairs={{0,16},{1,17},{2,18},{3,19},{4,20},{5,21},{6,22},{7,23},{8,24},{9,... | collective-permute-start | bytes 52232 | tf_op jit(solution)/shard_map/ppermute | solution.py:29
  178.0 4.6 collective-permute-start.8
  182.6 6.8 collective-permute-start.10
  189.4 4.6 collective-permute-start.12
  194.0 6.7 collective-permute-start.14
  442.4 56.6 %collective-permute-start.28 = (bf16[16,1024]{1,0:T(8,128)(2,1)S(1)}, bf16[16,1024]{1,0:T(8,128)(2,1)S(1)}, u32[]{:S(2)}, u32[]{:S(2)}) collective-permute-start(bf16[16,1024]{1,0:T(8,128)(2,1)S(1)} %get-tuple-element.221), channel_id=1, source_target_pairs={{0,1},{1,2},{2,3},{3,4},{4,5},{5,6},{6,7},{7,8},{8,9},{9,10},{10,1... | collective-permute-start | bytes 98312 | tf_op jit(solution)/shard_map/ppermute | solution.py:20
  445.9 53.8 %collective-permute-start.29 = (bf16[16,1024]{1,0:T(8,128)(2,1)S(1)}, bf16[16,1024]{1,0:T(8,128)(2,1)S(1)}, u32[]{:S(2)}, u32[]{:S(2)}) collective-permute-start(bf16[16,1024]{1,0:T(8,128)(2,1)S(1)} %get-tuple-element.221), channel_id=1, source_target_pairs={{1,0},{2,1},{3,2},{4,3},{5,4},{6,5},{7,6},{8,7},{9,8},{10,9},{11,1... | collective-permute-start | bytes 98312 | tf_op jit(solution)/shard_map/ppermute | solution.py:21
  447.9 157.8 %copy-start.7 = (f32[2,2,8,512]{3,2,0,1:T(8,128)}, f32[2,2,8,512]{3,2,0,1:T(8,128)S(1)}, u32[]{:S(2)}) copy-start(f32[2,2,8,512]{3,2,0,1:T(8,128)S(1)} %copy.29) | copy-start | bytes 196612
  448.8 16.5 %collective-permute-start.20 = (f32[16,256]{1,0:T(8,128)S(1)}, f32[16,256]{1,0:T(8,128)S(1)}, u32[]{:S(2)}, u32[]{:S(2)}) collective-permute-start(f32[16,256]{1,0:T(8,128)S(1)} %fusion.106), channel_id=1, source_target_pairs={{0,2},{1,3},{2,0},{3,1},{4,6},{5,7},{6,4},{7,5},{8,10},{9,11},{10,... | collective-permute-start | bytes 49160 | tf_op jit(solution)/shard_map/ppermute | solution.py:29
  451.8 23.4 %collective-permute-start.21 = (f32[16,256]{1,0:T(8,128)S(1)}, f32[16,256]{1,0:T(8,128)S(1)}, u32[]{:S(2)}, u32[]{:S(2)}) collective-permute-start(f32[16,256]{1,0:T(8,128)S(1)} %fusion.98), channel_id=1, source_target_pairs={{0,4},{1,5},{2,6},{3,7},{4,0},{5,1},{6,2},{7,3},{8,12},{9,13},{10,... | collective-permute-start | bytes 49160 | tf_op jit(solution)/shard_map/ppermute | solution.py:29
  460.9 17.6 %collective-permute-start.22 = (f32[16,256]{1,0:T(8,128)S(1)}, f32[16,256]{1,0:T(8,128)S(1)}, u32[]{:S(2)}, u32[]{:S(2)}) collective-permute-start(f32[16,256]{1,0:T(8,128)S(1)} %fusion.99), channel_id=1, source_target_pairs={{0,8},{1,9},{2,10},{3,11},{4,12},{5,13},{6,14},{7,15},{8,0},{9,1},... | collective-permute-start | bytes 49160 | tf_op jit(solution)/shard_map/ppermute | solution.py:29
  465.3 20.2 %collective-permute-start.23 = (f32[16,256]{1,0:T(8,128)S(1)}, f32[16,256]{1,0:T(8,128)S(1)}, u32[]{:S(2)}, u32[]{:S(2)}) collective-permute-start(f32[16,256]{1,0:T(8,128)S(1)} %fusion.100), channel_id=1, source_target_pairs={{0,16},{1,17},{2,18},{3,19},{4,20},{5,21},{6,22},{7,23},{8,24},{9,... | collective-permute-start | bytes 49160 | tf_op jit(solution)/shard_map/ppermute | solution.py:29
  475.1 13.9 %collective-permute-start.24 = (f32[16,256]{1,0:T(8,128)S(1)}, f32[16,256]{1,0:T(8,128)S(1)}, u32[]{:S(2)}, u32[]{:S(2)}) collective-permute-start(f32[16,256]{1,0:T(8,128)S(1)} %fusion.101), channel_id=1, source_target_pairs={{0,32},{1,33},{2,34},{3,35},{4,36},{5,37},{6,38},{7,39},{8,40},{9,... | collective-permute-start | bytes 49160 | tf_op jit(solution)/shard_map/ppermute | solution.py:29
  478.5 16.3 %collective-permute-start.25 = (f32[16,256]{1,0:T(8,128)S(1)}, f32[16,256]{1,0:T(8,128)S(1)}, u32[]{:S(2)}, u32[]{:S(2)}) collective-permute-start(f32[16,256]{1,0:T(8,128)S(1)} %fusion.102), channel_id=1, source_target_pairs={{0,64},{1,65},{2,66},{3,67},{4,68},{5,69},{6,70},{7,71},{8,72},{9,... | collective-permute-start | bytes 49160 | tf_op jit(solution)/shard_map/ppermute | solution.py:29
  485.5 10.7 %collective-permute-start.26 = (f32[16,256]{1,0:T(8,128)S(1)}, f32[16,256]{1,0:T(8,128)S(1)}, u32[]{:S(2)}, u32[]{:S(2)}) collective-permute-start(f32[16,256]{1,0:T(8,128)S(1)} %fusion.103), channel_id=1, source_target_pairs={{0,128},{1,129},{2,130},{3,131},{4,132},{5,133},{6,134},{7,135},{8... | collective-permute-start | bytes 49160 | tf_op jit(solution)/shard_map/ppermute | solution.py:29
  489.1 8.6 %collective-permute-start.27 = (f32[16,256]{1,0:T(8,128)S(1)}, f32[16,256]{1,0:T(8,128)S(1)}, u32[]{:S(2)}, u32[]{:S(2)}) collective-permute-start(f32[16,256]{1,0:T(8,128)S(1)} %fusion.104), channel_id=1, source_target_pairs={{0,256},{1,257},{2,258},{3,259},{4,260},{5,261},{6,262},{7,263},{8... | collective-permute-start | bytes 49160 | tf_op jit(solution)/shard_map/ppermute | solution.py:29
  (48 other events, 374.1 us)
where the time goes:
time: 712 us; the launch traced here: 706 us
  blocking collectives  416 us (58%)
  starting transfers between devices  133 us (19%)
  matrix products  63.5 us (9%)
  waiting for transfers between devices  44.4 us (6%)
  local copies, waits for them, and re-layouts  25.8 us (4%)
  other arithmetic  17.6 us (2%)
    psum x2, blocking collectives, norms_of(): return lax.psum(jnp.sum(values * values, axis=1), 'loc')  214 us
    ppermute x24, starting transfers between devices, partner(): return lax.ppermute(value, axis, pairs)  112 us
    psum x1, blocking collectives, shards(): alpha = norm_now / lax.psum(jnp.sum(direction * image, axis=1), 'loc')  104 us
    psum x1, blocking collectives, shards(): lax.psum(jnp.sum(solution * slope_image, axis=1), 'loc') / point_total  98.2 us
    ppermute x24, waiting for transfers between devices, partner(): return lax.ppermute(value, axis, pairs)  44.4 us
    dot_general x28, matrix products, contract_rows(): lax.dot_general(vectors, matrix, (((1,), (1,)), ((), ())), preferred_elem...  41 us
    dot_general x16, matrix products, far_part(): jnp.dot(mixed_half, bases[level_id], preferred_element_type=jnp.float32)  15.1 us
  transfers between devices with their start and end apart: 30, of which 13 were waited for; matrix products, arithmetic and copies ran while one was open for 12% of the time, Pallas kernels for 0%

commit v1 on v0

v1 whole, which is shorter than its diff:
```python
import functools

import jax
import jax.numpy as jnp
from jax import lax
from jax.experimental import pallas as pl
from jax.experimental.pallas import tpu as pltpu
from jax.sharding import PartitionSpec as P

F32 = jnp.float32
BF = jnp.bfloat16
LOG2E = 1.4426950408889634
STRIDE = 4
LANES = 128
VROWS = 48
CROWS = 24
MESH = pl.DeviceIdType.MESH


def split2(x):
    hi = x.astype(BF)
    return hi, (x - hi.astype(F32)).astype(BF)


def split3(x):
    hi = x.astype(BF).astype(F32)
    rest = x - hi
    mid = rest.astype(BF).astype(F32)
    return hi, mid, rest - mid


def row_ids(shape):
    return lax.broadcasted_iota(jnp.int32, shape, 0)


def left_side(pts, scale, extra=None):
    rows = row_ids(pts.shape)
    square = scale * jnp.sum(pts * pts, axis=0, keepdims=True)
    full = jnp.where(rows < 3, -2.0 * scale * pts, jnp.where(rows == 3, square, jnp.where(rows == 4, scale, 0.0)))
    hi, mid, low = split3(full)
    parts = [hi, hi, hi, mid, mid, mid, low, low, low]
    if extra is not None:
        parts.append(extra)
    filler = jnp.zeros((LANES - 8 * len(parts), pts.shape[1]), F32)
    return jnp.concatenate(parts + [filler], axis=0)


def right_side(pts):
    rows = row_ids(pts.shape)
    square = jnp.sum(pts * pts, axis=0, keepdims=True)
    full = jnp.where(rows < 3, pts, jnp.where(rows == 3, 1.0, jnp.where(rows == 4, square, 0.0)))
    hi, mid, low = split3(full)
    filler = jnp.zeros((LANES - 72, pts.shape[1]), F32)
    return jnp.concatenate([hi, mid, low] * 3 + [filler], axis=0).astype(BF)


def matern(square, want_slope):
    square = jnp.maximum(square, 1e-30)
    scaled = square * lax.rsqrt(square)
    decay = jnp.exp2(scaled * (-LOG2E))
    first = scaled * decay
    if want_slope:
        return decay + first, scaled * first
    return decay + first


def dot(a, b):
    return jnp.dot(a, b, preferred_element_type=F32)


def dot_t(a, b):
    return lax.dot_general(a, b, (((1,), (1,)), ((), ())), preferred_element_type=F32)


def pack(columns):
    lanes = lax.broadcasted_iota(jnp.int32, (16, LANES), 1)
    rows = row_ids((16, LANES))
    total = jnp.zeros((16, LANES), F32)
    for k, column in enumerate(columns):
        total = jnp.where(lanes == rows + 16 * k, column, total)
    return jnp.sum(total, axis=0, keepdims=True)


def unpack(line, k):
    lanes = lax.broadcasted_iota(jnp.int32, (16, LANES), 1)
    rows = row_ids((16, LANES))
    return jnp.sum(jnp.where(lanes == rows + 16 * k, line, 0.0), axis=1, keepdims=True)


def row_dot(a, b):
    return jnp.sum(a * b, axis=1, keepdims=True)


def kernel(
    bits, groups, pts_ref, r0_ref, skel_ref, len_ref, far_ref, sig_ref, noise_ref,
    sol_ref, res_ref, slope_ref, trace_ref,
    p8, vec, qvec, nbp, nbr, at, a_near, a_far, b_own, kbuf, fbuf, psel, prec, chi, clo, grp,
    cs1, cr1, cs2, cr2, acc_k, acc_s, far_acc, q_buf, rs_buf, red_a, red_b,
    nb_send, nb_recv, q_send, q_recv, sk_send, sk_recv, c1_send, c1_recv, c2_send, c2_recv,
    ra_send, ra_recv, rb_send, rb_recv,
):
    n = 2**bits
    levels, rank = skel_ref.shape
    rows = pts_ref.shape[1]
    tile = rank
    tiles = rows // tile
    far_scale = 1.0 / (rank * rank * levels)
    me = lax.axis_index("loc")
    flip = [2**b * (1 - 2 * ((me // 2**b) % 2)) for b in range(bits)]
    right = (me + 1) % n
    left = (me + n - 1) % n
    group_a, group_b = groups

    def peers(group):
        found = []
        for d in range(1, 2 ** len(group)):
            found.append(me + sum(flip[b] for i, b in enumerate(group) if (d >> i) & 1))
        return found

    peers_a, peers_b = peers(group_a), peers(group_b)
    barrier = pltpu.get_barrier_semaphore()
    for peer in peers_a + peers_b + [left, right]:
        pl.semaphore_signal(barrier, inc=1, device_id=(peer,), device_id_type=MESH)

    def send(src, dst, ssem, rsem, peer):
        copy = pltpu.make_async_remote_copy(
            src_ref=src, dst_ref=dst, send_sem=ssem, recv_sem=rsem, device_id=(peer,), device_id_type=MESH
        )
        copy.start()
        return copy

    pending = []

    p8[...] = jnp.zeros_like(p8)
    p8[0:3, :] = pts_ref[...]
    raw = p8[...]
    centre = raw[:, 0:1]
    own = raw - centre
    near_scale = 3.0 / jnp.full((1, rows), len_ref[0] * len_ref[0], F32)
    far_scale2 = 3.0 / jnp.full((1, rows), far_ref[0] * far_ref[0], F32)
    b_own[...] = right_side(own)
    a_near[1] = left_side(own, near_scale).T.astype(BF)
    at[...] = left_side(own, far_scale2, raw).T
    picks = []
    for o in range(STRIDE):
        part = at[pl.ds(o, rank, stride=STRIDE), :]
        a_far[o] = part.astype(BF)
        picks.append(part.T[72:80, :])

    offs = skel_ref[...] - STRIDE * lax.broadcasted_iota(jnp.int32, skel_ref.shape, 1)

    def choose(level, values):
        off = offs[level : level + 1, :]
        result = values[0]
        for o in range(1, STRIDE):
            result = jnp.where(off == o, values[o], result)
        return result

    for level in range(levels):
        psel[level] = choose(level, picks)

    r0 = r0_ref[...]
    hi, low = split2(r0)
    vec[1, 0:16, :] = hi
    vec[1, 16:32, :] = low
    marks = jnp.where(row_ids((16, rows)) == 0, 1.0, 0.0)
    vec[1, 32:48, :] = marks.astype(BF)

    def far_chunk(o, carry):
        left_part = a_far[o]
        for j in range(tiles):
            cols = pl.ds(j * tile, tile)
            fbuf[o, :, cols] = matern(dot(left_part, b_own[:, cols]), False).astype(BF)
        grp[o] = dot_t(vec[1], fbuf[o])
        return carry

    lax.fori_loop(0, STRIDE, far_chunk, 0)

    parts = [grp[o] for o in range(STRIDE)]
    parts = [
        jnp.concatenate([g[0:16] + g[16:32], g[32:40]], axis=0)
        for g in parts
    ]
    for level in range(levels):
        cs1[level] = choose(level, parts)

    pl.semaphore_wait(barrier, len(peers_a) + len(peers_b) + 2)

    nb = [
        send(pts_ref, nbp.at[0], nb_send.at[0], nb_recv.at[0], right),
        send(pts_ref, nbp.at[1], nb_send.at[1], nb_recv.at[1], left),
        send(r0_ref, nbr.at[0], nb_send.at[2], nb_recv.at[2], right),
        send(r0_ref, nbr.at[1], nb_send.at[3], nb_recv.at[3], left),
    ]
    sk, c1 = [], []
    for level in range(levels):
        peer = me + flip[level + 1]
        sk.append(send(psel.at[level], prec.at[level], sk_send.at[level], sk_recv.at[level], peer))
        c1.append(send(cs1.at[level], cr1.at[level], c1_send.at[level], c1_recv.at[level], peer))
    pending += nb + sk + c1

    acc_k[...] = jnp.zeros_like(acc_k)
    acc_s[...] = jnp.zeros_like(acc_s)

    def near_block(slot):
        def chunk(i, carry):
            at_rows = pl.ds(pl.multiple_of(i * tile, tile), tile)
            left_part = a_near[slot, at_rows, :]
            head = vec[slot, :, at_rows]
            for j in range(tiles):
                cols = pl.ds(j * tile, tile)
                value, slope = matern(dot(left_part, b_own[:, cols]), True)
                value = value.astype(BF)
                kbuf[slot, at_rows, cols] = value
                acc_k[:, cols] += dot(head, value)
                acc_s[:, cols] += dot(head[0:16], slope.astype(BF))
            return carry

        lax.fori_loop(0, tiles, chunk, 0)

    near_block(1)
    valid = [jnp.where(me > 0, 1.0, 0.0), jnp.where(me < n - 1, 1.0, 0.0)]
    for side, slot in ((0, 0), (1, 2)):
        nb[side].wait_recv()
        nb[2 + side].wait_recv()
        p8[0:3, :] = nbp[side]
        a_near[slot] = left_side(p8[...] - centre, near_scale).T.astype(BF)
        hi, low = split2(nbr[side] * valid[side])
        vec[slot, 0:16, :] = hi
        vec[slot, 16:32, :] = low
        vec[slot, 32:48, :] = (marks * valid[side]).astype(BF)
        near_block(slot)

    side_scale = far_scale2[:, 0:rank]
    for level in range(levels):
        sk[level].wait_recv()
        a_side = left_side(prec[level] - centre, side_scale).T.astype(BF)
        b_side = right_side(psel[level] - centre)
        hi, low = split2(matern(dot(a_side, b_side), False))
        chi[level] = hi
        clo[level] = low

    def far_part(copies, received, rounded):
        count = received.shape[1]
        sums = [jnp.zeros((count, rank), F32) for _ in range(STRIDE)]
        for level in range(levels):
            copies[level].wait_recv()
            hi, low = split2(received[level])
            mixed = dot(hi, chi[level]) + dot(low, chi[level]) + dot(hi, clo[level])
            off = offs[level : level + 1, :]
            for o in range(STRIDE):
                sums[o] = sums[o] + jnp.where(off == o, mixed, 0.0)
        total = jnp.zeros((count, rows), F32)
        for o in range(STRIDE):
            hi, low = split2(sums[o])
            total = total + dot(hi, fbuf[o]) + dot(low, fbuf[o])
        return far_scale * total

    far_now = far_part(c1, cr1, True)
    near_now = acc_k[...]
    sig, noise = sig_ref[0], noise_ref[0]
    row_sums = near_now[32:33] + far_now[16:17]
    image = noise * r0 + sig * (near_now[0:16] + near_now[16:32] + far_now[0:16] + row_sums * r0)
    slope_image = sig * acc_s[...]
    slope_ref[...] = slope_image
    q_buf[...] = image
    rs_buf[...] = jnp.broadcast_to(row_sums, rs_buf.shape)
    hi, low = split2(image)
    qvec[1, 0:16, :] = hi
    qvec[1, 16:32, :] = low

    qs = [
        send(qvec.at[1], qvec.at[0], q_send.at[0], q_recv.at[0], right),
        send(qvec.at[1], qvec.at[2], q_send.at[1], q_recv.at[1], left),
    ]

    def start_reduce(step, line):
        red_a[step, 0] = line
        return [
            send(red_a.at[step, 0], red_a.at[step, d + 1], ra_send.at[step, d], ra_recv.at[step, d], peer)
            for d, peer in enumerate(peers_a)
        ]

    def halve(values):
        while values.shape[0] > 1:
            half = values.shape[0] // 2
            values = values[:half] + values[half:]
        return values[0]

    def middle_reduce(step, copies):
        for copy in copies:
            copy.wait_recv()
        red_b[step, 0] = halve(red_a[step])
        return [
            send(red_b.at[step, 0], red_b.at[step, d + 1], rb_send.at[step, d], rb_recv.at[step, d], peer)
            for d, peer in enumerate(peers_b)
        ]

    def end_reduce(step, copies):
        for copy in copies:
            copy.wait_recv()
        return halve(red_b[step])

    line = pack([row_dot(r0, r0), row_dot(r0, image), row_dot(r0, slope_image)])
    first_a = start_reduce(0, line)

    parts = []
    for o in range(STRIDE):
        g = dot_t(qvec[1], fbuf[o])
        parts.append(g[0:16] + g[16:32])
    for level in range(levels):
        cs2[level] = choose(level, parts)
    c2 = [
        send(cs2.at[level], cr2.at[level], c2_send.at[level], c2_recv.at[level], me + flip[level + 1])
        for level in range(levels)
    ]
    pending += qs + first_a + c2

    acc2 = dot(qvec[1], kbuf[1])
    first_b = middle_reduce(0, first_a)
    pending += first_b
    for side, slot in ((0, 0), (1, 2)):
        qs[side].wait_recv()
        acc2 = acc2 + valid[side] * dot(qvec[slot], kbuf[slot])
    far_now = far_part(c2, cr2, False)
    image = q_buf[...]
    second = noise * image + sig * (acc2[0:16] + acc2[16:32] + far_now + rs_buf[0:1, :] * image)

    line = end_reduce(0, first_b)
    norm0, inner0, start_slope = unpack(line, 0), unpack(line, 1), unpack(line, 2)
    alpha0 = norm0 / inner0
    slope_image = slope_ref[...]
    r0 = r0_ref[...]
    r1 = r0 - alpha0 * image
    r1_image = image - alpha0 * second
    line = pack(
        [
            row_dot(r1, r1),
            row_dot(r1, r1_image),
            row_dot(r1, image) + row_dot(r0, r1_image),
            row_dot(r1, slope_image),
        ]
    )
    second_a = start_reduce(1, line)
    second_b = middle_reduce(1, second_a)
    line = end_reduce(1, second_b)
    pending += second_a + second_b
    norm1, inner1, cross1, slope1 = [unpack(line, k) for k in range(4)]
    beta = norm1 / norm0
    inner1 = inner1 + beta * (cross1 + beta * inner0)
    alpha1 = norm1 / inner1
    direction = r1 + beta * r0
    sol_ref[...] = alpha0 * r0 + alpha1 * direction
    res_ref[...] = r1 - alpha1 * (r1_image + beta * image)
    trace = (alpha0 * start_slope + alpha1 * (slope1 + beta * start_slope)) * (1.0 / (n * rows))
    trace_ref[...] = pack([trace])
    for copy in pending:
        copy.wait_send()


def shards(points, right_sides, skeleton, lengthscale, far_length, signal, noise_var):
    n = lax.axis_size("loc")
    bits = n.bit_length() - 1
    rows = points.shape[1]
    levels, rank = skeleton.shape
    split = min(5, bits // 2 + 1)
    groups = (tuple(range(split)), tuple(range(split, bits)))
    size_a, size_b = 2 ** len(groups[0]), 2 ** len(groups[1])
    vmem = pl.BlockSpec(memory_space=pltpu.VMEM)
    smem = pl.BlockSpec(memory_space=pltpu.SMEM)
    dma = pltpu.SemaphoreType.DMA
    scratch = [
        pltpu.VMEM((8, rows), F32),
        pltpu.VMEM((3, VROWS, rows), BF),
        pltpu.VMEM((3, 32, rows), BF),
        pltpu.VMEM((2, 3, rows), F32),
        pltpu.VMEM((2, 16, rows), F32),
        pltpu.VMEM((rows, LANES), F32),
        pltpu.VMEM((3, rows, LANES), BF),
        pltpu.VMEM((STRIDE, rank, LANES), BF),
        pltpu.VMEM((LANES, rows), BF),
        pltpu.VMEM((3, rows, rows), BF),
        pltpu.VMEM((STRIDE, rank, rows), BF),
        pltpu.VMEM((levels, 8, rank), F32),
        pltpu.VMEM((levels, 8, rank), F32),
        pltpu.VMEM((levels, rank, rank), BF),
        pltpu.VMEM((levels, rank, rank), BF),
        pltpu.VMEM((STRIDE, VROWS, rank), F32),
        pltpu.VMEM((levels, CROWS, rank), F32),
        pltpu.VMEM((levels, CROWS, rank), F32),
        pltpu.VMEM((levels, 16, rank), F32),
        pltpu.VMEM((levels, 16, rank), F32),
        pltpu.VMEM((VROWS, rows), F32),
        pltpu.VMEM((16, rows), F32),
        pltpu.VMEM((16, rows), F32),
        pltpu.VMEM((16, rows), F32),
        pltpu.VMEM((8, rows), F32),
        pltpu.VMEM((2, size_a, 1, LANES), F32),
        pltpu.VMEM((2, size_b, 1, LANES), F32),
        dma((4,)), dma((4,)), dma((2,)), dma((2,)),
        dma((levels,)), dma((levels,)), dma((levels,)), dma((levels,)), dma((levels,)), dma((levels,)),
        dma((2, size_a - 1)), dma((2, size_a - 1)), dma((2, size_b - 1)), dma((2, size_b - 1)),
    ]
    block = jax.ShapeDtypeStruct(right_sides.shape, F32)
    outs = pl.pallas_call(
        functools.partial(kernel, bits, groups),
        out_shape=(block, block, block, jax.ShapeDtypeStruct((1, LANES), F32)),
        in_specs=[vmem] * 3 + [smem] * 4,
        out_specs=(vmem,) * 4,
        scratch_shapes=scratch,
        compiler_params=pltpu.CompilerParams(collective_id=0, has_side_effects=True, vmem_limit_bytes=48 * 2**20),
        name="cg",
    )(points, right_sides, skeleton, lengthscale, far_length, signal, noise_var)
    return outs[0], outs[1], outs[2], outs[3][0, : right_sides.shape[0]]


def solution(mesh):
    placed = (P(None, "loc"), P(None, "loc"), P(None, "loc"), P(), P(), P(), P())
    return jax.shard_map(
        shards,
        mesh=mesh,
        in_specs=placed,
        out_specs=(P(None, "loc"), P(None, "loc"), P(None, "loc"), P()),
        check_vma=False,
    )
```

time: 712 us -> 67.2 us (0.09)
  blocking collectives: 416 us -> 0 us
  starting transfers between devices: 133 us -> 0 us
  matrix products: 63.5 us -> 0 us
  Pallas kernels: 0 us -> 59 us
  waiting for transfers between devices: 44.4 us -> 0 us
  local copies, waits for them, and re-layouts: 25.8 us -> 4.65 us
  other arithmetic: 17.6 us -> 0 us
    psum x4 -> x0, blocking collectives: 416 us -> none  [the longest x2 214 us: norms_of(): return lax.psum(jnp.sum(values * values, axis=1), 'loc')]
    ppermute x30 -> x0, starting transfers between devices: 133 us -> none  [the longest x24 112 us: partner(): return lax.ppermute(value, axis, pairs)]
    dot_general x60 -> x0, matrix products: 63.5 us -> none  [the longest x28 41 us: contract_rows(): lax.dot_general(vectors, matrix, (((1,), (1,)), ((), ())), preferred_elem...]
    pallas_call x0 -> x1, Pallas kernels: none -> 59 us  [shards(): pl.pallas_call(functools.partial(kernel, bits, groups), out_shape=(block,...]
    ppermute x30 -> x0, waiting for transfers between devices: 44.4 us -> none  [the longest x24 44.4 us: partner(): return lax.ppermute(value, axis, pairs)]
    gather x8 -> x0, local copies, waits for them, and re-layouts: 13.7 us -> none  [shards(): jnp.take(points, skeleton[level_id], axis=1)]
    dynamic_update_slice x6 -> x0, other arithmetic: 13.1 us -> none  [make_block(): lax.scan(one_tile, back_init, (tile_pts_all, tile_pts_all))]
    slice x33 -> x0, local copies, waits for them, and re-layouts: 7.95 us -> none  [the longest x29 5.37 us: kernel_pair(): diff_a = row_pts[0][:, None] - col_pts[0][None, :]]
  transfers between devices with their start and end apart: 30 -> 0, of which waited for: 13 -> 0; matrix products, arithmetic and copies ran while one was open for 12% -> 0% of each run, Pallas kernels for 0% -> 0%
where the time goes in v1:
time: 67.2 us; the launch traced here: 66.9 us
  Pallas kernels  59 us (88%)
  local copies, waits for them, and re-layouts  4.65 us (7%)
  between operations  3.23 us (5%)
    pallas_call x1, Pallas kernels, shards(): pl.pallas_call(functools.partial(kernel, bits, groups), out_shape=(block,...  59 us
    unnamed x9, local copies, waits for them, and re-layouts  4.13 us

profile of v1, /device:TPU:1, one launch (start us, length us, event | category | flops | bytes accessed | tf_op | source)
XLA Modules:
  0.0 66.9 jit_solution(18263750529044910563)
XLA Ops:
  3.2 0.0 copy-start
  3.2 0.8 %copy-done = f32[16,1024]{1,0:T(8,128)S(1)} copy-done((f32[16,1024]{1,0:T(8,128)S(1)}, f32[16,1024]{1,0:T(8,128)}, u32[]{:S(2)}) %copy-start) | copy-done | bytes 65560
  4.1 0.0 copy-start.1
  4.1 0.7 %copy-done.1 = f32[3,1024]{1,0:T(4,128)S(1)} copy-done((f32[3,1024]{1,0:T(4,128)S(1)}, f32[3,1024]{1,0:T(4,128)}, u32[]{:S(2)}) %copy-start.1) | copy-done | bytes 12312
  4.8 0.0 copy-start.2
  4.8 0.7 %copy-done.2 = s32[8,256]{1,0:T(8,128)S(1)} copy-done((s32[8,256]{1,0:T(8,128)S(1)}, s32[8,256]{1,0:T(8,128)}, u32[]{:S(2)}) %copy-start.2) | copy-done | bytes 8216
  5.5 59.0 %cg.1 = (f32[16,1024]{1,0:T(8,128)S(1)}, f32[16,1024]{1,0:T(8,128)S(1)}, f32[16,1024]{1,0:T(8,128)S(1)}, f32[1,128]{1,0:T(1,128)S(1)}) custom-call(f32[3,1024]{1,0:T(4,128)S(1)} %copy-done.1, f32[16,1024]{1,0:T(8,128)S(1)} %copy-done, s32[8,256]{1,0:T(8,128)S(1)} %copy-done.2, f32[1]{0:T(128)S(6)} %copy.14.len_ref, f32[1]{0:T(128)S(6)} %copy.15.far_ref, ...), custom_call_target="tpu_custom_call" | custom-call | tf_op jit(solution)/shard_map/cg/pallas_call | solution.py:405
  64.5 0.5 slice_bitcast_fusion
  65.0 0.6 copy.18
  65.6 0.6 copy.19
  66.2 0.6 copy.20
Async XLA Ops:
  3.2 0.8 %copy-start = (f32[16,1024]{1,0:T(8,128)S(1)}, f32[16,1024]{1,0:T(8,128)}, u32[]{:S(2)}) copy-start(f32[16,1024]{1,0:T(8,128)} %r0_ref.1) | copy-start | bytes 196612
  4.1 0.7 %copy-start.1 = (f32[3,1024]{1,0:T(4,128)S(1)}, f32[3,1024]{1,0:T(4,128)}, u32[]{:S(2)}) copy-start(f32[3,1024]{1,0:T(4,128)} %pts_ref.1) | copy-start | bytes 36868
  4.8 0.7 %copy-start.2 = (s32[8,256]{1,0:T(8,128)S(1)}, s32[8,256]{1,0:T(8,128)}, u32[]{:S(2)}) copy-start(s32[8,256]{1,0:T(8,128)} %skel_ref.1) | copy-start | bytes 24580

commit v2 on v1

--- a/solution.py
+++ b/solution.py
@@ -13,7 +13,6 @@
 STRIDE = 4
 LANES = 128
 VROWS = 48
-CROWS = 24
 MESH = pl.DeviceIdType.MESH
 
 
@@ -92,10 +91,10 @@
 
 
 def kernel(
-    bits, groups, pts_ref, r0_ref, skel_ref, len_ref, far_ref, sig_ref, noise_ref,
-    sol_ref, res_ref, slope_ref, trace_ref,
-    p8, vec, qvec, nbp, nbr, at, a_near, a_far, b_own, kbuf, fbuf, psel, prec, chi, clo, grp,
-    cs1, cr1, cs2, cr2, acc_k, acc_s, far_acc, q_buf, rs_buf, red_a, red_b,
+    bits, groups, pts_hbm, r0_hbm, skel_hbm, len_ref, far_ref, sig_ref, noise_ref,
+    r1_ref, r1_image_ref, q_buf, slope_ref, first_ref, last_ref,
+    pts_ref, r0_ref, skel_ref, in_sem, p8, vec, qvec, nbp, nbr, at, a_near, a_far, b_own, kbuf, fbuf, psel, prec, chi, clo, grp,
+    cs1, cr1, cs2, cr2, acc_k, rs_buf, red_a, red_b,
     nb_send, nb_recv, q_send, q_recv, sk_send, sk_recv, c1_send, c1_recv, c2_send, c2_recv,
     ra_send, ra_recv, rb_send, rb_recv,
 ):
@@ -105,6 +104,12 @@
     tile = rank
     tiles = rows // tile
     far_scale = 1.0 / (rank * rank * levels)
+    loads = [
+        pltpu.make_async_copy(src, dst, in_sem.at[i])
+        for i, (src, dst) in enumerate(((pts_hbm, pts_ref), (skel_hbm, skel_ref), (r0_hbm, r0_ref)))
+    ]
+    for load in loads:
+        load.start()
     me = lax.axis_index("loc")
     flip = [2**b * (1 - 2 * ((me // 2**b) % 2)) for b in range(bits)]
     right = (me + 1) % n
@@ -129,9 +134,10 @@
         copy.start()
         return copy
 
-    pending = []
+    order = sorted(range(levels), key=lambda level: -(2**level if level < 4 else 2 ** (level % 2)))
 
     p8[...] = jnp.zeros_like(p8)
+    loads[0].wait()
     p8[0:3, :] = pts_ref[...]
     raw = p8[...]
     centre = raw[:, 0:1]
@@ -147,6 +153,7 @@
         a_far[o] = part.astype(BF)
         picks.append(part.T[72:80, :])
 
+    loads[1].wait()
     offs = skel_ref[...] - STRIDE * lax.broadcasted_iota(jnp.int32, skel_ref.shape, 1)
 
     def choose(level, values):
@@ -157,8 +164,9 @@
         return result
 
     for level in range(levels):
-        psel[level] = choose(level, picks)
-
+        psel[level, 0:3, :] = choose(level, picks)[0:3]
+
+    loads[2].wait()
     r0 = r0_ref[...]
     hi, low = split2(r0)
     vec[1, 0:16, :] = hi
@@ -177,30 +185,29 @@
     lax.fori_loop(0, STRIDE, far_chunk, 0)
 
     parts = [grp[o] for o in range(STRIDE)]
-    parts = [
-        jnp.concatenate([g[0:16] + g[16:32], g[32:40]], axis=0)
-        for g in parts
-    ]
-    for level in range(levels):
-        cs1[level] = choose(level, parts)
+    sums = [g[0:16] + g[16:32] for g in parts]
+    ones = [g[32:33] for g in parts]
+    for level in order:
+        cs1[level] = choose(level, sums)
+        psel[level, 3:4, :] = choose(level, ones)
 
     pl.semaphore_wait(barrier, len(peers_a) + len(peers_b) + 2)
 
-    nb = [
-        send(pts_ref, nbp.at[0], nb_send.at[0], nb_recv.at[0], right),
-        send(pts_ref, nbp.at[1], nb_send.at[1], nb_recv.at[1], left),
-        send(r0_ref, nbr.at[0], nb_send.at[2], nb_recv.at[2], right),
-        send(r0_ref, nbr.at[1], nb_send.at[3], nb_recv.at[3], left),
-    ]
-    sk, c1 = [], []
-    for level in range(levels):
+    sk, c1 = {}, {}
+    for i, level in enumerate(order):
         peer = me + flip[level + 1]
-        sk.append(send(psel.at[level], prec.at[level], sk_send.at[level], sk_recv.at[level], peer))
-        c1.append(send(cs1.at[level], cr1.at[level], c1_send.at[level], c1_recv.at[level], peer))
-    pending += nb + sk + c1
+        sk[level] = send(psel.at[level], prec.at[level], sk_send.at[level], sk_recv.at[level], peer)
+        c1[level] = send(cs1.at[level], cr1.at[level], c1_send.at[level], c1_recv.at[level], peer)
+        if i == min(1, levels - 1):
+            nb = [
+                send(pts_ref, nbp.at[0], nb_send.at[0], nb_recv.at[0], right),
+                send(pts_ref, nbp.at[1], nb_send.at[1], nb_recv.at[1], left),
+                send(r0_ref, nbr.at[0], nb_send.at[2], nb_recv.at[2], right),
+                send(r0_ref, nbr.at[1], nb_send.at[3], nb_recv.at[3], left),
+            ]
 
     acc_k[...] = jnp.zeros_like(acc_k)
-    acc_s[...] = jnp.zeros_like(acc_s)
+    slope_ref[...] = jnp.zeros_like(slope_ref)
 
     def near_block(slot):
         def chunk(i, carry):
@@ -213,7 +220,7 @@
                 value = value.astype(BF)
                 kbuf[slot, at_rows, cols] = value
                 acc_k[:, cols] += dot(head, value)
-                acc_s[:, cols] += dot(head[0:16], slope.astype(BF))
+                slope_ref[:, cols] += dot(head[0:16], slope.astype(BF))
             return carry
 
         lax.fori_loop(0, tiles, chunk, 0)
@@ -232,36 +239,45 @@
         near_block(slot)
 
     side_scale = far_scale2[:, 0:rank]
-    for level in range(levels):
+
+    def centred(four):
+        full = jnp.concatenate([four, jnp.zeros_like(four)], axis=0)
+        return jnp.where(row_ids(full.shape) < 3, full - centre, 0.0)
+
+    for level in reversed(order):
         sk[level].wait_recv()
-        a_side = left_side(prec[level] - centre, side_scale).T.astype(BF)
-        b_side = right_side(psel[level] - centre)
+        a_side = left_side(centred(prec[level]), side_scale).T.astype(BF)
+        b_side = right_side(centred(psel[level]))
         hi, low = split2(matern(dot(a_side, b_side), False))
         chi[level] = hi
         clo[level] = low
 
-    def far_part(copies, received, rounded):
-        count = received.shape[1]
+    def far_part(copies, received, with_ones):
+        count = 24 if with_ones else 16
         sums = [jnp.zeros((count, rank), F32) for _ in range(STRIDE)]
-        for level in range(levels):
+        for level in reversed(order):
             copies[level].wait_recv()
-            hi, low = split2(received[level])
-            mixed = dot(hi, chi[level]) + dot(low, chi[level]) + dot(hi, clo[level])
+            coef = received[level]
+            if with_ones:
+                tail = jnp.where(row_ids((8, rank)) == 0, prec[level, 3:4, :], 0.0)
+                coef = jnp.concatenate([coef, tail], axis=0)
+            hi, low = split2(coef)
+            both = dot(jnp.concatenate([hi, low], axis=0), chi[level])
+            mixed = both[:count] + both[count:] + dot(hi, clo[level])
             off = offs[level : level + 1, :]
             for o in range(STRIDE):
                 sums[o] = sums[o] + jnp.where(off == o, mixed, 0.0)
-        total = jnp.zeros((count, rows), F32)
+        total = jnp.zeros((2 * count, rows), F32)
         for o in range(STRIDE):
-            hi, low = split2(sums[o])
-            total = total + dot(hi, fbuf[o]) + dot(low, fbuf[o])
-        return far_scale * total
+            total = total + dot(jnp.concatenate(split2(sums[o]), axis=0), fbuf[o])
+        return far_scale * (total[:count] + total[count:])
 
     far_now = far_part(c1, cr1, True)
     near_now = acc_k[...]
     sig, noise = sig_ref[0], noise_ref[0]
     row_sums = near_now[32:33] + far_now[16:17]
     image = noise * r0 + sig * (near_now[0:16] + near_now[16:32] + far_now[0:16] + row_sums * r0)
-    slope_image = sig * acc_s[...]
+    slope_image = sig * slope_ref[...]
     slope_ref[...] = slope_image
     q_buf[...] = image
     rs_buf[...] = jnp.broadcast_to(row_sums, rs_buf.shape)
@@ -308,17 +324,16 @@
     for o in range(STRIDE):
         g = dot_t(qvec[1], fbuf[o])
         parts.append(g[0:16] + g[16:32])
-    for level in range(levels):
+    c2 = {}
+    for level in order:
         cs2[level] = choose(level, parts)
-    c2 = [
-        send(cs2.at[level], cr2.at[level], c2_send.at[level], c2_recv.at[level], me + flip[level + 1])
-        for level in range(levels)
-    ]
-    pending += qs + first_a + c2
+        peer = me + flip[level + 1]
+        c2[level] = send(cs2.at[level], cr2.at[level], c2_send.at[level], c2_recv.at[level], peer)
 
     acc2 = dot(qvec[1], kbuf[1])
     first_b = middle_reduce(0, first_a)
-    pending += first_b
+    for copy in nb + list(sk.values()) + list(c1.values()):
+        copy.wait_send()
     for side, slot in ((0, 0), (1, 2)):
         qs[side].wait_recv()
         acc2 = acc2 + valid[side] * dot(qvec[slot], kbuf[slot])
@@ -327,8 +342,8 @@
     second = noise * image + sig * (acc2[0:16] + acc2[16:32] + far_now + rs_buf[0:1, :] * image)
 
     line = end_reduce(0, first_b)
-    norm0, inner0, start_slope = unpack(line, 0), unpack(line, 1), unpack(line, 2)
-    alpha0 = norm0 / inner0
+    first_ref[...] = line
+    alpha0 = unpack(line, 0) / unpack(line, 1)
     slope_image = slope_ref[...]
     r0 = r0_ref[...]
     r1 = r0 - alpha0 * image
@@ -342,20 +357,43 @@
         ]
     )
     second_a = start_reduce(1, line)
+    r1_ref[...] = r1
+    r1_image_ref[...] = r1_image
+    for copy in qs + first_a + list(c2.values()) + first_b:
+        copy.wait_send()
     second_b = middle_reduce(1, second_a)
-    line = end_reduce(1, second_b)
-    pending += second_a + second_b
-    norm1, inner1, cross1, slope1 = [unpack(line, k) for k in range(4)]
+    for copy in second_a:
+        copy.wait_send()
+    last_ref[...] = end_reduce(1, second_b)
+    for copy in second_b:
+        copy.wait_send()
+
+
+def finish(scale, r1_ref, r1_image_ref, q_ref, slope_ref, first_ref, last_ref,
+           sol_hbm, res_hbm, slope_hbm, trace_hbm, sol, res, trace_buf, sem):
+    outs = [
+        pltpu.make_async_copy(src, dst, sem.at[i])
+        for i, (src, dst) in enumerate(
+            ((slope_ref, slope_hbm), (sol, sol_hbm), (res, res_hbm), (trace_buf, trace_hbm))
+        )
+    ]
+    outs[0].start()
+    first, last = first_ref[...], last_ref[...]
+    norm0, inner0, start_slope = unpack(first, 0), unpack(first, 1), unpack(first, 2)
+    norm1, inner1, cross1, slope1 = [unpack(last, k) for k in range(4)]
+    alpha0 = norm0 / inner0
     beta = norm1 / norm0
-    inner1 = inner1 + beta * (cross1 + beta * inner0)
-    alpha1 = norm1 / inner1
-    direction = r1 + beta * r0
-    sol_ref[...] = alpha0 * r0 + alpha1 * direction
-    res_ref[...] = r1 - alpha1 * (r1_image + beta * image)
-    trace = (alpha0 * start_slope + alpha1 * (slope1 + beta * start_slope)) * (1.0 / (n * rows))
-    trace_ref[...] = pack([trace])
-    for copy in pending:
-        copy.wait_send()
+    alpha1 = norm1 / (inner1 + beta * (cross1 + beta * inner0))
+    r1, q = r1_ref[...], q_ref[...]
+    sol[...] = (alpha0 + alpha1 * beta) * (r1 + alpha0 * q) + alpha1 * r1
+    outs[1].start()
+    res[...] = r1 - alpha1 * (r1_image_ref[...] + beta * q)
+    outs[2].start()
+    trace = (alpha0 * start_slope + alpha1 * (slope1 + beta * start_slope)) * scale
+    trace_buf[...] = pack([trace])[:, 0:16]
+    outs[3].start()
+    for out in outs:
+        out.wait()
 
 
 def shards(points, right_sides, skeleton, lengthscale, far_length, signal, noise_var):
@@ -369,7 +407,12 @@
     vmem = pl.BlockSpec(memory_space=pltpu.VMEM)
     smem = pl.BlockSpec(memory_space=pltpu.SMEM)
     dma = pltpu.SemaphoreType.DMA
+    hbm = pl.BlockSpec(memory_space=pltpu.HBM)
     scratch = [
+        pltpu.VMEM((3, rows), F32),
+        pltpu.VMEM((16, rows), F32),
+        pltpu.VMEM((levels, rank), jnp.int32),
+        dma((3,)),
         pltpu.VMEM((8, rows), F32),
         pltpu.VMEM((3, VROWS, rows), BF),
         pltpu.VMEM((3, 32, rows), BF),
@@ -381,19 +424,16 @@
         pltpu.VMEM((LANES, rows), BF),
         pltpu.VMEM((3, rows, rows), BF),
         pltpu.VMEM((STRIDE, rank, rows), BF),
-        pltpu.VMEM((levels, 8, rank), F32),
-        pltpu.VMEM((levels, 8, rank), F32),
+        pltpu.VMEM((levels, 4, rank), F32),
+        pltpu.VMEM((levels, 4, rank), F32),
         pltpu.VMEM((levels, rank, rank), BF),
         pltpu.VMEM((levels, rank, rank), BF),
         pltpu.VMEM((STRIDE, VROWS, rank), F32),
-        pltpu.VMEM((levels, CROWS, rank), F32),
-        pltpu.VMEM((levels, CROWS, rank), F32),
+        pltpu.VMEM((levels, 16, rank), F32),
+        pltpu.VMEM((levels, 16, rank), F32),
         pltpu.VMEM((levels, 16, rank), F32),
         pltpu.VMEM((levels, 16, rank), F32),
         pltpu.VMEM((VROWS, rows), F32),
-        pltpu.VMEM((16, rows), F32),
-        pltpu.VMEM((16, rows), F32),
-        pltpu.VMEM((16, rows), F32),
         pltpu.VMEM((8, rows), F32),
         pltpu.VMEM((2, size_a, 1, LANES), F32),
         pltpu.VMEM((2, size_b, 1, LANES), F32),
@@ -402,16 +442,29 @@
         dma((2, size_a - 1)), dma((2, size_a - 1)), dma((2, size_b - 1)), dma((2, size_b - 1)),
     ]
     block = jax.ShapeDtypeStruct(right_sides.shape, F32)
-    outs = pl.pallas_call(
+    row = jax.ShapeDtypeStruct((1, LANES), F32)
+    parts = pl.pallas_call(
         functools.partial(kernel, bits, groups),
-        out_shape=(block, block, block, jax.ShapeDtypeStruct((1, LANES), F32)),
-        in_specs=[vmem] * 3 + [smem] * 4,
-        out_specs=(vmem,) * 4,
+        out_shape=(block,) * 4 + (row,) * 2,
+        in_specs=[hbm] * 3 + [smem] * 4,
+        out_specs=(vmem,) * 6,
         scratch_shapes=scratch,
-        compiler_params=pltpu.CompilerParams(collective_id=0, has_side_effects=True, vmem_limit_bytes=48 * 2**20),
+        compiler_params=pltpu.CompilerParams(collective_id=0, has_side_effects=True, vmem_limit_bytes=56_200_000),
         name="cg",
     )(points, right_sides, skeleton, lengthscale, far_length, signal, noise_var)
-    return outs[0], outs[1], outs[2], outs[3][0, : right_sides.shape[0]]
+    probes = right_sides.shape[0]
+    outs = pl.pallas_call(
+        functools.partial(finish, 1.0 / (n * rows)),
+        out_shape=(block, block, block, jax.ShapeDtypeStruct((1, probes), F32)),
+        in_specs=[vmem] * 6,
+        out_specs=(hbm,) * 4,
+        scratch_shapes=[
+            pltpu.VMEM(right_sides.shape, F32), pltpu.VMEM(right_sides.shape, F32), pltpu.VMEM((1, probes), F32), dma((4,)),
+        ],
+        compiler_params=pltpu.CompilerParams(vmem_limit_bytes=2 * 2**20),
+        name="finish",
+    )(*parts)
+    return outs[0], outs[1], outs[2], outs[3].reshape(probes)
 
 
 def solution(mesh):

time: 67.2 us -> 64.1 us (0.954)
  local copies, waits for them, and re-layouts: 4.65 us -> 1.41 us
    unnamed x9 -> x4, local copies, waits for them, and re-layouts: 4.13 us -> 1.41 us
    pallas_call x0 -> x1, Pallas kernels: none -> 0.8 us  [shards(): pl.pallas_call(functools.partial(finish, 1.0 / (n * rows)), out_shape=(bl...]
where the time goes in v2:
time: 64.1 us; the launch traced here: 63.9 us
  Pallas kernels  59.2 us (92%)
  between operations  3.23 us (5%)
  local copies, waits for them, and re-layouts  1.41 us (2%)
    pallas_call x1, Pallas kernels, shards(): pl.pallas_call(functools.partial(kernel, bits, groups), out_shape=(block,...  58.4 us
    unnamed x4, local copies, waits for them, and re-layouts  1.41 us

profile of v2, /device:TPU:1, one launch (start us, length us, event | category | flops | bytes accessed | tf_op | source)
XLA Modules:
  0.0 63.9 jit_solution(12976809706014634663)
XLA Ops:
  3.2 0.0 copy-start
  3.2 0.7 %copy-done = f32[3,1024]{1,0:T(4,128)S(1)} copy-done((f32[3,1024]{1,0:T(4,128)S(1)}, f32[3,1024]{1,0:T(4,128)}, u32[]{:S(2)}) %copy-start) | copy-done | bytes 12312
  3.9 0.0 copy-start.1
  3.9 0.7 %copy-done.1 = s32[8,256]{1,0:T(8,128)S(1)} copy-done((s32[8,256]{1,0:T(8,128)S(1)}, s32[8,256]{1,0:T(8,128)}, u32[]{:S(2)}) %copy-start.1) | copy-done | bytes 8216
  4.6 58.4 %cg.1 = (f32[16,1024]{1,0:T(8,128)S(1)}, f32[16,1024]{1,0:T(8,128)S(1)}, f32[16,1024]{1,0:T(8,128)S(1)}, f32[16,1024]{1,0:T(8,128)S(1)}, f32[1,128]{1,0:T(1,128)S(1)}, /*index=5*/f32[1,128]{1,0:T(1,128)S(1)}) custom-call(f32[3,1024]{1,0:T(4,128)S(1)} %copy-done, f32[16,1024]{1,0:T(8,128)} %r0_hbm.1, s32[8,256]{1,0:T(8,128)S(1)} %copy-done.1, ...), custom_call_target="tpu_custom_call" | custom-call | tf_op jit(solution)/shard_map/cg/pallas_call | solution.py:446
  63.1 0.8 %finish.1 = (f32[16,1024]{1,0:T(8,128)}, f32[16,1024]{1,0:T(8,128)}, f32[16,1024]{1,0:T(8,128)}, f32[1,16]{1,0:T(1,128)}) custom-call(f32[16,1024]{1,0:T(8,128)S(1)} %get-tuple-element.14.r1_ref, f32[16,1024]{1,0:T(8,128)S(1)} %get-tuple-element.15.r1_image_ref, f32[16,1024]{1,0:T(8,128)S(1)} %get-tuple-element.16.q_ref, ...), custom_call_target="tpu_custom_call" | custom-call | tf_op jit(solution)/shard_map/finish/pallas_call | solution.py:456
Async XLA Ops:
  3.2 0.7 %copy-start = (f32[3,1024]{1,0:T(4,128)S(1)}, f32[3,1024]{1,0:T(4,128)}, u32[]{:S(2)}) copy-start(f32[3,1024]{1,0:T(4,128)} %pts_hbm.1) | copy-start | bytes 36868
  3.9 0.7 %copy-start.1 = (s32[8,256]{1,0:T(8,128)S(1)}, s32[8,256]{1,0:T(8,128)}, u32[]{:S(2)}) copy-start(s32[8,256]{1,0:T(8,128)} %skel_hbm.1) | copy-start | bytes 24580

commit v3 on v2

--- a/solution.py
+++ b/solution.py
@@ -134,6 +134,33 @@
         copy.start()
         return copy
 
+    def start_reduce(step, line):
+        red_a[step, 0] = line
+        return [
+            send(red_a.at[step, 0], red_a.at[step, d + 1], ra_send.at[step, d], ra_recv.at[step, d], peer)
+            for d, peer in enumerate(peers_a)
+        ]
+
+    def halve(values):
+        while values.shape[0] > 1:
+            half = values.shape[0] // 2
+            values = values[:half] + values[half:]
+        return values[0]
+
+    def middle_reduce(step, copies):
+        for copy in copies:
+            copy.wait_recv()
+        red_b[step, 0] = halve(red_a[step])
+        return [
+            send(red_b.at[step, 0], red_b.at[step, d + 1], rb_send.at[step, d], rb_recv.at[step, d], peer)
+            for d, peer in enumerate(peers_b)
+        ]
+
+    def end_reduce(step, copies):
+        for copy in copies:
+            copy.wait_recv()
+        return halve(red_b[step])
+
     order = sorted(range(levels), key=lambda level: -(2**level if level < 4 else 2 ** (level % 2)))
 
     p8[...] = jnp.zeros_like(p8)
@@ -225,7 +252,24 @@
 
         lax.fori_loop(0, tiles, chunk, 0)
 
-    near_block(1)
+    def own_tiles(use):
+        for i in range(tiles):
+            for j in range(i, tiles):
+                use(pl.ds(i * tile, tile), pl.ds(j * tile, tile), i == j)
+
+    def own_near(rows_i, rows_j, diagonal):
+        value, slope = matern(dot(a_near[1, rows_i, :], b_own[:, rows_j]), True)
+        value, slope = value.astype(BF), slope.astype(BF)
+        kbuf[1, rows_i, rows_j] = value
+        head = vec[1, :, rows_i]
+        acc_k[:, rows_j] += dot(head, value)
+        slope_ref[:, rows_j] += dot(head[0:16], slope)
+        if not diagonal:
+            head = vec[1, :, rows_j]
+            acc_k[:, rows_i] += dot_t(head, value)
+            slope_ref[:, rows_i] += dot_t(head[0:16], slope)
+
+    own_tiles(own_near)
     valid = [jnp.where(me > 0, 1.0, 0.0), jnp.where(me < n - 1, 1.0, 0.0)]
     for side, slot in ((0, 0), (1, 2)):
         nb[side].wait_recv()
@@ -238,19 +282,28 @@
         vec[slot, 32:48, :] = (marks * valid[side]).astype(BF)
         near_block(slot)
 
+    near_now = acc_k[...]
+    sig, noise = sig_ref[0], noise_ref[0]
+    rough = noise * r0 + sig * (near_now[0:16] + near_now[16:32] + near_now[32:33] * r0)
+    first_a = start_reduce(0, pack([row_dot(r0, r0), row_dot(r0, rough)]))
+
     side_scale = far_scale2[:, 0:rank]
 
     def centred(four):
         full = jnp.concatenate([four, jnp.zeros_like(four)], axis=0)
         return jnp.where(row_ids(full.shape) < 3, full - centre, 0.0)
 
-    for level in reversed(order):
-        sk[level].wait_recv()
-        a_side = left_side(centred(prec[level]), side_scale).T.astype(BF)
-        b_side = right_side(centred(psel[level]))
-        hi, low = split2(matern(dot(a_side, b_side), False))
-        chi[level] = hi
-        clo[level] = low
+    arrivals = order[::-1]
+    for start in range(0, levels, 4):
+        batch = arrivals[start : start + 4]
+        for level in batch:
+            sk[level].wait_recv()
+        for level in batch:
+            a_side = left_side(centred(prec[level]), side_scale).T.astype(BF)
+            b_side = right_side(centred(psel[level]))
+            hi, low = split2(matern(dot(a_side, b_side), False))
+            chi[level] = hi
+            clo[level] = low
 
     def far_part(copies, received, with_ones):
         count = 24 if with_ones else 16
@@ -274,7 +327,6 @@
 
     far_now = far_part(c1, cr1, True)
     near_now = acc_k[...]
-    sig, noise = sig_ref[0], noise_ref[0]
     row_sums = near_now[32:33] + far_now[16:17]
     image = noise * r0 + sig * (near_now[0:16] + near_now[16:32] + far_now[0:16] + row_sums * r0)
     slope_image = sig * slope_ref[...]
@@ -290,35 +342,7 @@
         send(qvec.at[1], qvec.at[2], q_send.at[1], q_recv.at[1], left),
     ]
 
-    def start_reduce(step, line):
-        red_a[step, 0] = line
-        return [
-            send(red_a.at[step, 0], red_a.at[step, d + 1], ra_send.at[step, d], ra_recv.at[step, d], peer)
-            for d, peer in enumerate(peers_a)
-        ]
-
-    def halve(values):
-        while values.shape[0] > 1:
-            half = values.shape[0] // 2
-            values = values[:half] + values[half:]
-        return values[0]
-
-    def middle_reduce(step, copies):
-        for copy in copies:
-            copy.wait_recv()
-        red_b[step, 0] = halve(red_a[step])
-        return [
-            send(red_b.at[step, 0], red_b.at[step, d + 1], rb_send.at[step, d], rb_recv.at[step, d], peer)
-            for d, peer in enumerate(peers_b)
-        ]
-
-    def end_reduce(step, copies):
-        for copy in copies:
-            copy.wait_recv()
-        return halve(red_b[step])
-
-    line = pack([row_dot(r0, r0), row_dot(r0, image), row_dot(r0, slope_image)])
-    first_a = start_reduce(0, line)
+    norm0, start_slope = row_dot(r0, r0), row_dot(r0, slope_image)
 
     parts = []
     for o in range(STRIDE):
@@ -330,7 +354,16 @@
         peer = me + flip[level + 1]
         c2[level] = send(cs2.at[level], cr2.at[level], c2_send.at[level], c2_recv.at[level], peer)
 
-    acc2 = dot(qvec[1], kbuf[1])
+    acc_k[...] = jnp.zeros_like(acc_k)
+
+    def own_again(rows_i, rows_j, diagonal):
+        value = kbuf[1, rows_i, rows_j]
+        acc_k[0:32, rows_j] += dot(qvec[1, :, rows_i], value)
+        if not diagonal:
+            acc_k[0:32, rows_i] += dot_t(qvec[1, :, rows_j], value)
+
+    own_tiles(own_again)
+    acc2 = acc_k[0:32, :]
     first_b = middle_reduce(0, first_a)
     for copy in nb + list(sk.values()) + list(c1.values()):
         copy.wait_send()
@@ -343,16 +376,19 @@
 
     line = end_reduce(0, first_b)
     first_ref[...] = line
-    alpha0 = unpack(line, 0) / unpack(line, 1)
+    step = unpack(line, 0) / unpack(line, 1)
     slope_image = slope_ref[...]
     r0 = r0_ref[...]
-    r1 = r0 - alpha0 * image
-    r1_image = image - alpha0 * second
+    r1 = r0 - step * image
+    r1_image = image - step * second
     line = pack(
         [
+            norm0,
+            row_dot(r0, r1),
             row_dot(r1, r1),
+            row_dot(r0, r1_image),
             row_dot(r1, r1_image),
-            row_dot(r1, image) + row_dot(r0, r1_image),
+            start_slope,
             row_dot(r1, slope_image),
         ]
     )
@@ -379,15 +415,25 @@
     ]
     outs[0].start()
     first, last = first_ref[...], last_ref[...]
-    norm0, inner0, start_slope = unpack(first, 0), unpack(first, 1), unpack(first, 2)
-    norm1, inner1, cross1, slope1 = [unpack(last, k) for k in range(4)]
-    alpha0 = norm0 / inner0
+    step = unpack(first, 0) / unpack(first, 1)
+    norm0, along, square, image_along, image_own, start_slope, own_slope = [unpack(last, k) for k in range(7)]
+    share = along / norm0
+    gain = norm0 / (norm0 - along)
+    inner0 = (norm0 - along) / step
+    mixed = (along - square) / step + image_along
+    norm1 = gain * gain * (square - share * along)
+    inner1 = gain * gain * (image_own - share * mixed + share * share * inner0)
+    cross1 = gain * (mixed - 2.0 * share * inner0)
+    slope1 = gain * (own_slope - share * start_slope)
+    alpha0 = step * gain
     beta = norm1 / norm0
     alpha1 = norm1 / (inner1 + beta * (cross1 + beta * inner0))
-    r1, q = r1_ref[...], q_ref[...]
-    sol[...] = (alpha0 + alpha1 * beta) * (r1 + alpha0 * q) + alpha1 * r1
+    q = q_ref[...]
+    r0 = r1_ref[...] + step * q
+    r1 = gain * (r1_ref[...] - share * r0)
+    sol[...] = (alpha0 + alpha1 * beta) * r0 + alpha1 * r1
     outs[1].start()
-    res[...] = r1 - alpha1 * (r1_image_ref[...] + beta * q)
+    res[...] = r1 - alpha1 * (gain * (r1_image_ref[...] - share * q) + beta * q)
     outs[2].start()
     trace = (alpha0 * start_slope + alpha1 * (slope1 + beta * start_slope)) * scale
     trace_buf[...] = pack([trace])[:, 0:16]

time: 64.1 us -> 60.5 us (0.944)
  Pallas kernels: 59.2 us -> 55.6 us
    pallas_call x1, Pallas kernels: 58.4 us -> 54.8 us  [shards(): pl.pallas_call(functools.partial(kernel, bits, groups), out_shape=(block,...]
where the time goes in v3:
time: 60.5 us; the launch traced here: 60.2 us
  Pallas kernels  55.6 us (92%)
  between operations  3.23 us (5%)
  local copies, waits for them, and re-layouts  1.41 us (2%)
    pallas_call x1, Pallas kernels, shards(): pl.pallas_call(functools.partial(kernel, bits, groups), out_shape=(block,...  54.8 us
    unnamed x4, local copies, waits for them, and re-layouts  1.41 us

profile of v3, /device:TPU:1, one launch (start us, length us, event | category | flops | bytes accessed | tf_op | source)
XLA Modules:
  0.0 60.2 jit_solution(12422426410549007560)
XLA Ops:
  3.2 0.0 copy-start
  3.2 0.7 %copy-done = f32[3,1024]{1,0:T(4,128)S(1)} copy-done((f32[3,1024]{1,0:T(4,128)S(1)}, f32[3,1024]{1,0:T(4,128)}, u32[]{:S(2)}) %copy-start) | copy-done | bytes 12312
  3.9 0.0 copy-start.1
  3.9 0.7 %copy-done.1 = s32[8,256]{1,0:T(8,128)S(1)} copy-done((s32[8,256]{1,0:T(8,128)S(1)}, s32[8,256]{1,0:T(8,128)}, u32[]{:S(2)}) %copy-start.1) | copy-done | bytes 8216
  4.6 54.8 %cg.1 = (f32[16,1024]{1,0:T(8,128)S(1)}, f32[16,1024]{1,0:T(8,128)S(1)}, f32[16,1024]{1,0:T(8,128)S(1)}, f32[16,1024]{1,0:T(8,128)S(1)}, f32[1,128]{1,0:T(1,128)S(1)}, /*index=5*/f32[1,128]{1,0:T(1,128)S(1)}) custom-call(f32[3,1024]{1,0:T(4,128)S(1)} %copy-done, f32[16,1024]{1,0:T(8,128)} %r0_hbm.1, s32[8,256]{1,0:T(8,128)S(1)} %copy-done.1, ...), custom_call_target="tpu_custom_call" | custom-call | tf_op jit(solution)/shard_map/cg/pallas_call | solution.py:492
  59.4 0.8 %finish.1 = (f32[16,1024]{1,0:T(8,128)}, f32[16,1024]{1,0:T(8,128)}, f32[16,1024]{1,0:T(8,128)}, f32[1,16]{1,0:T(1,128)}) custom-call(f32[16,1024]{1,0:T(8,128)S(1)} %get-tuple-element.14.r1_ref, f32[16,1024]{1,0:T(8,128)S(1)} %get-tuple-element.15.r1_image_ref, f32[16,1024]{1,0:T(8,128)S(1)} %get-tuple-element.16.q_ref, ...), custom_call_target="tpu_custom_call" | custom-call | tf_op jit(solution)/shard_map/finish/pallas_call | solution.py:502
Async XLA Ops:
  3.2 0.7 %copy-start = (f32[3,1024]{1,0:T(4,128)S(1)}, f32[3,1024]{1,0:T(4,128)}, u32[]{:S(2)}) copy-start(f32[3,1024]{1,0:T(4,128)} %pts_hbm.1) | copy-start | bytes 36868
  3.9 0.7 %copy-start.1 = (s32[8,256]{1,0:T(8,128)S(1)}, s32[8,256]{1,0:T(8,128)}, u32[]{:S(2)}) copy-start(s32[8,256]{1,0:T(8,128)} %skel_hbm.1) | copy-start | bytes 24580

commit v4 on v3

--- a/solution.py
+++ b/solution.py
@@ -124,7 +124,7 @@
 
     peers_a, peers_b = peers(group_a), peers(group_b)
     barrier = pltpu.get_barrier_semaphore()
-    for peer in peers_a + peers_b + [left, right]:
+    for peer in peers_a[::-1] + peers_b + [left, right]:
         pl.semaphore_signal(barrier, inc=1, device_id=(peer,), device_id_type=MESH)
 
     def send(src, dst, ssem, rsem, peer):
@@ -172,7 +172,6 @@
     near_scale = 3.0 / jnp.full((1, rows), len_ref[0] * len_ref[0], F32)
     far_scale2 = 3.0 / jnp.full((1, rows), far_ref[0] * far_ref[0], F32)
     b_own[...] = right_side(own)
-    a_near[1] = left_side(own, near_scale).T.astype(BF)
     at[...] = left_side(own, far_scale2, raw).T
     picks = []
     for o in range(STRIDE):
@@ -269,6 +268,7 @@
             acc_k[:, rows_i] += dot_t(head, value)
             slope_ref[:, rows_i] += dot_t(head[0:16], slope)
 
+    a_near[1] = left_side(own, near_scale).T.astype(BF)
     own_tiles(own_near)
     valid = [jnp.where(me > 0, 1.0, 0.0), jnp.where(me < n - 1, 1.0, 0.0)]
     for side, slot in ((0, 0), (1, 2)):
@@ -320,9 +320,8 @@
             off = offs[level : level + 1, :]
             for o in range(STRIDE):
                 sums[o] = sums[o] + jnp.where(off == o, mixed, 0.0)
-        total = jnp.zeros((2 * count, rows), F32)
-        for o in range(STRIDE):
-            total = total + dot(jnp.concatenate(split2(sums[o]), axis=0), fbuf[o])
+        halves = [jnp.concatenate(split2(part), axis=0) for part in sums]
+        total = dot(jnp.concatenate(halves, axis=1), fbuf[...].reshape(rows, rows))
         return far_scale * (total[:count] + total[count:])
 
     far_now = far_part(c1, cr1, True)
@@ -345,8 +344,9 @@
     norm0, start_slope = row_dot(r0, r0), row_dot(r0, slope_image)
 
     parts = []
+    both = dot_t(qvec[1], fbuf[...].reshape(rows, rows))
     for o in range(STRIDE):
-        g = dot_t(qvec[1], fbuf[o])
+        g = both[:, o * rank : (o + 1) * rank]
         parts.append(g[0:16] + g[16:32])
     c2 = {}
     for level in order:
@@ -497,7 +497,7 @@
         scratch_shapes=scratch,
         compiler_params=pltpu.CompilerParams(collective_id=0, has_side_effects=True, vmem_limit_bytes=56_200_000),
         name="cg",
-    )(points, right_sides, skeleton, lengthscale, far_length, signal, noise_var)
+    )(*[pltpu.with_memory_space_constraint(a, pltpu.HBM) for a in (points, right_sides, skeleton)], lengthscale, far_length, signal, noise_var)
     probes = right_sides.shape[0]
     outs = pl.pallas_call(
         functools.partial(finish, 1.0 / (n * rows)),

time: 60.5 us -> 59 us (0.975)
  local copies, waits for them, and re-layouts: 1.41 us -> 0 us
    unnamed x4 -> x0, local copies, waits for them, and re-layouts: 1.41 us -> none
where the time goes in v4:
time: 59 us; the launch traced here: 58.8 us
  Pallas kernels  55.5 us (94%)
  between operations  3.22 us (5%)
    pallas_call x1, Pallas kernels, shards(): pl.pallas_call(functools.partial(kernel, bits, groups), out_shape=(block,...  54.7 us

profile of v4, /device:TPU:1, one launch (start us, length us, event | category | flops | bytes accessed | tf_op | source)
XLA Modules:
  0.0 58.8 jit_solution(439637283632933102)
XLA Ops:
  3.2 54.7 %cg.1 = (f32[16,1024]{1,0:T(8,128)S(1)}, f32[16,1024]{1,0:T(8,128)S(1)}, f32[16,1024]{1,0:T(8,128)S(1)}, f32[16,1024]{1,0:T(8,128)S(1)}, f32[1,128]{1,0:T(1,128)S(1)}, /*index=5*/f32[1,128]{1,0:T(1,128)S(1)}) custom-call(f32[3,1024]{1,0:T(4,128)} %pts_hbm.1, f32[16,1024]{1,0:T(8,128)} %r0_hbm.1, s32[8,256]{1,0:T(8,128)} %skel_hbm.1, f32[1]{0:T(128)S(6)} %copy.11.len_ref, ...), custom_call_target="tpu_custom_call" | custom-call | tf_op jit(solution)/shard_map/cg/pallas_call | solution.py:492
  57.9 0.8 %finish.1 = (f32[16,1024]{1,0:T(8,128)}, f32[16,1024]{1,0:T(8,128)}, f32[16,1024]{1,0:T(8,128)}, f32[1,16]{1,0:T(1,128)}) custom-call(f32[16,1024]{1,0:T(8,128)S(1)} %get-tuple-element.14.r1_ref, f32[16,1024]{1,0:T(8,128)S(1)} %get-tuple-element.15.r1_image_ref, f32[16,1024]{1,0:T(8,128)S(1)} %get-tuple-element.16.q_ref, ...), custom_call_target="tpu_custom_call" | custom-call | tf_op jit(solution)/shard_map/finish/pallas_call | solution.py:502

commit v5 on v4

--- a/solution.py
+++ b/solution.py
@@ -94,7 +94,7 @@
     bits, groups, pts_hbm, r0_hbm, skel_hbm, len_ref, far_ref, sig_ref, noise_ref,
     r1_ref, r1_image_ref, q_buf, slope_ref, first_ref, last_ref,
     pts_ref, r0_ref, skel_ref, in_sem, p8, vec, qvec, nbp, nbr, at, a_near, a_far, b_own, kbuf, fbuf, psel, prec, chi, clo, grp,
-    cs1, cr1, cs2, cr2, acc_k, rs_buf, red_a, red_b,
+    cs1, cr1, cs2, cr2, acc_k, rs_buf, basis, red_a, red_b,
     nb_send, nb_recv, q_send, q_recv, sk_send, sk_recv, c1_send, c1_recv, c2_send, c2_recv,
     ra_send, ra_recv, rb_send, rb_recv,
 ):
@@ -220,17 +220,24 @@
     pl.semaphore_wait(barrier, len(peers_a) + len(peers_b) + 2)
 
     sk, c1 = {}, {}
+
+    def send_coefs(level):
+        peer = me + flip[level + 1]
+        c1[level] = send(cs1.at[level], cr1.at[level], c1_send.at[level], c1_recv.at[level], peer)
+
     for i, level in enumerate(order):
+        if i < 2:
+            send_coefs(level)
         peer = me + flip[level + 1]
         sk[level] = send(psel.at[level], prec.at[level], sk_send.at[level], sk_recv.at[level], peer)
-        c1[level] = send(cs1.at[level], cr1.at[level], c1_send.at[level], c1_recv.at[level], peer)
-        if i == min(1, levels - 1):
-            nb = [
-                send(pts_ref, nbp.at[0], nb_send.at[0], nb_recv.at[0], right),
-                send(pts_ref, nbp.at[1], nb_send.at[1], nb_recv.at[1], left),
-                send(r0_ref, nbr.at[0], nb_send.at[2], nb_recv.at[2], right),
-                send(r0_ref, nbr.at[1], nb_send.at[3], nb_recv.at[3], left),
-            ]
+    nb = [
+        send(pts_ref, nbp.at[0], nb_send.at[0], nb_recv.at[0], right),
+        send(pts_ref, nbp.at[1], nb_send.at[1], nb_recv.at[1], left),
+        send(r0_ref, nbr.at[0], nb_send.at[2], nb_recv.at[2], right),
+        send(r0_ref, nbr.at[1], nb_send.at[3], nb_recv.at[3], left),
+    ]
+    for level in order[2:]:
+        send_coefs(level)
 
     acc_k[...] = jnp.zeros_like(acc_k)
     slope_ref[...] = jnp.zeros_like(slope_ref)
@@ -270,6 +277,27 @@
 
     a_near[1] = left_side(own, near_scale).T.astype(BF)
     own_tiles(own_near)
+
+    side_scale = far_scale2[:, 0:rank]
+
+    def centred(four):
+        full = jnp.concatenate([four, jnp.zeros_like(four)], axis=0)
+        return jnp.where(row_ids(full.shape) < 3, full - centre, 0.0)
+
+    arrivals = order[::-1]
+
+    def couplings(batch):
+        for level in batch:
+            sk[level].wait_recv()
+        for level in batch:
+            a_side = left_side(centred(prec[level]), side_scale).T.astype(BF)
+            b_side = right_side(centred(psel[level]))
+            hi, low = split2(matern(dot(a_side, b_side), False))
+            chi[level] = hi
+            clo[level] = low
+
+    couplings(arrivals[:4])
+
     valid = [jnp.where(me > 0, 1.0, 0.0), jnp.where(me < n - 1, 1.0, 0.0)]
     for side, slot in ((0, 0), (1, 2)):
         nb[side].wait_recv()
@@ -287,44 +315,34 @@
     rough = noise * r0 + sig * (near_now[0:16] + near_now[16:32] + near_now[32:33] * r0)
     first_a = start_reduce(0, pack([row_dot(r0, r0), row_dot(r0, rough)]))
 
-    side_scale = far_scale2[:, 0:rank]
-
-    def centred(four):
-        full = jnp.concatenate([four, jnp.zeros_like(four)], axis=0)
-        return jnp.where(row_ids(full.shape) < 3, full - centre, 0.0)
-
-    arrivals = order[::-1]
-    for start in range(0, levels, 4):
-        batch = arrivals[start : start + 4]
-        for level in batch:
-            sk[level].wait_recv()
-        for level in batch:
-            a_side = left_side(centred(prec[level]), side_scale).T.astype(BF)
-            b_side = right_side(centred(psel[level]))
-            hi, low = split2(matern(dot(a_side, b_side), False))
-            chi[level] = hi
-            clo[level] = low
-
-    def far_part(copies, received, with_ones):
-        count = 24 if with_ones else 16
-        sums = [jnp.zeros((count, rank), F32) for _ in range(STRIDE)]
-        for level in reversed(order):
-            copies[level].wait_recv()
-            coef = received[level]
-            if with_ones:
-                tail = jnp.where(row_ids((8, rank)) == 0, prec[level, 3:4, :], 0.0)
-                coef = jnp.concatenate([coef, tail], axis=0)
-            hi, low = split2(coef)
-            both = dot(jnp.concatenate([hi, low], axis=0), chi[level])
-            mixed = both[:count] + both[count:] + dot(hi, clo[level])
+    couplings(arrivals[4:])
+
+    def mix(copy, received, level, with_ones):
+        copy.wait_recv()
+        coef = received[level]
+        if with_ones:
+            tail = jnp.where(row_ids((8, rank)) == 0, prec[level, 3:4, :], 0.0)
+            coef = jnp.concatenate([coef, tail], axis=0)
+        count = coef.shape[0]
+        hi, low = split2(coef)
+        both = dot(jnp.concatenate([hi, low], axis=0), chi[level])
+        return both[:count] + both[count:] + dot(hi, clo[level])
+
+    def apply_halves(values, matrix):
+        total = dot(jnp.concatenate([jnp.concatenate(split2(v), axis=0) for v in values], axis=1), matrix)
+        count = total.shape[0] // 2
+        return far_scale * (total[:count] + total[count:])
+
+    def far_part(copies, received, with_ones, among):
+        sums = [jnp.zeros((24 if with_ones else 16, rank), F32) for _ in range(STRIDE)]
+        for level in among:
+            mixed = mix(copies[level], received, level, with_ones)
             off = offs[level : level + 1, :]
             for o in range(STRIDE):
                 sums[o] = sums[o] + jnp.where(off == o, mixed, 0.0)
-        halves = [jnp.concatenate(split2(part), axis=0) for part in sums]
-        total = dot(jnp.concatenate(halves, axis=1), fbuf[...].reshape(rows, rows))
-        return far_scale * (total[:count] + total[count:])
-
-    far_now = far_part(c1, cr1, True)
+        return apply_halves(sums, fbuf[...].reshape(rows, rows))
+
+    far_now = far_part(c1, cr1, True, arrivals)
     near_now = acc_k[...]
     row_sums = near_now[32:33] + far_now[16:17]
     image = noise * r0 + sig * (near_now[0:16] + near_now[16:32] + far_now[0:16] + row_sums * r0)
@@ -370,7 +388,13 @@
     for side, slot in ((0, 0), (1, 2)):
         qs[side].wait_recv()
         acc2 = acc2 + valid[side] * dot(qvec[slot], kbuf[slot])
-    far_now = far_part(c2, cr2, False)
+    last = arrivals[-1]
+    column = offs.astype(F32).T[:, last : last + 1]
+    picked = jnp.zeros((rank, rows), F32)
+    for o in range(STRIDE):
+        picked = jnp.where(column == o, fbuf[o].astype(F32), picked)
+    basis[...] = picked.astype(BF)
+    far_now = far_part(c2, cr2, False, arrivals[:-1])
     image = q_buf[...]
     second = noise * image + sig * (acc2[0:16] + acc2[16:32] + far_now + rs_buf[0:1, :] * image)
 
@@ -380,21 +404,14 @@
     slope_image = slope_ref[...]
     r0 = r0_ref[...]
     r1 = r0 - step * image
+    r1_ref[...] = r1
+    along, square, own_slope = row_dot(r0, r1), row_dot(r1, r1), row_dot(r1, slope_image)
     r1_image = image - step * second
-    line = pack(
-        [
-            norm0,
-            row_dot(r0, r1),
-            row_dot(r1, r1),
-            row_dot(r0, r1_image),
-            row_dot(r1, r1_image),
-            start_slope,
-            row_dot(r1, slope_image),
-        ]
-    )
+    mixed = mix(c2[last], cr2, last, False)
+    r1_image = r1_image - (step * sig) * apply_halves([mixed], basis[...])
+    r1_image_ref[...] = r1_image
+    line = pack([norm0, along, square, row_dot(r0, r1_image), row_dot(r1, r1_image), start_slope, own_slope])
     second_a = start_reduce(1, line)
-    r1_ref[...] = r1
-    r1_image_ref[...] = r1_image
     for copy in qs + first_a + list(c2.values()) + first_b:
         copy.wait_send()
     second_b = middle_reduce(1, second_a)
@@ -481,6 +498,7 @@
         pltpu.VMEM((levels, 16, rank), F32),
         pltpu.VMEM((VROWS, rows), F32),
         pltpu.VMEM((8, rows), F32),
+        pltpu.VMEM((rank, rows), BF),
         pltpu.VMEM((2, size_a, 1, LANES), F32),
         pltpu.VMEM((2, size_b, 1, LANES), F32),
         dma((4,)), dma((4,)), dma((2,)), dma((2,)),

time: 59 us -> 59.2 us (level)
  no operation moved by 1% of the time
where the time goes in v5:
time: 59.2 us; the launch traced here: 58.9 us
  Pallas kernels  55.7 us (94%)
  between operations  3.22 us (5%)
    pallas_call x1, Pallas kernels, shards(): pl.pallas_call(functools.partial(kernel, bits, groups), out_shape=(block,...  54.9 us

profile of v5, /device:TPU:1, one launch (start us, length us, event | category | flops | bytes accessed | tf_op | source)
XLA Modules:
  0.0 58.9 jit_solution(4334317421437002831)
XLA Ops:
  3.2 54.9 %cg.1 = (f32[16,1024]{1,0:T(8,128)S(1)}, f32[16,1024]{1,0:T(8,128)S(1)}, f32[16,1024]{1,0:T(8,128)S(1)}, f32[16,1024]{1,0:T(8,128)S(1)}, f32[1,128]{1,0:T(1,128)S(1)}, /*index=5*/f32[1,128]{1,0:T(1,128)S(1)}) custom-call(f32[3,1024]{1,0:T(4,128)} %pts_hbm.1, f32[16,1024]{1,0:T(8,128)} %r0_hbm.1, s32[8,256]{1,0:T(8,128)} %skel_hbm.1, f32[1]{0:T(128)S(6)} %copy.11.len_ref, ...), custom_call_target="tpu_custom_call" | custom-call | tf_op jit(solution)/shard_map/cg/pallas_call | solution.py:510
  58.1 0.8 %finish.1 = (f32[16,1024]{1,0:T(8,128)}, f32[16,1024]{1,0:T(8,128)}, f32[16,1024]{1,0:T(8,128)}, f32[1,16]{1,0:T(1,128)}) custom-call(f32[16,1024]{1,0:T(8,128)S(1)} %get-tuple-element.14.r1_ref, f32[16,1024]{1,0:T(8,128)S(1)} %get-tuple-element.15.r1_image_ref, f32[16,1024]{1,0:T(8,128)S(1)} %get-tuple-element.16.q_ref, ...), custom_call_target="tpu_custom_call" | custom-call | tf_op jit(solution)/shard_map/finish/pallas_call | solution.py:520

commit v6 on v5

--- a/solution.py
+++ b/solution.py
@@ -226,18 +226,16 @@
         c1[level] = send(cs1.at[level], cr1.at[level], c1_send.at[level], c1_recv.at[level], peer)
 
     for i, level in enumerate(order):
-        if i < 2:
-            send_coefs(level)
         peer = me + flip[level + 1]
         sk[level] = send(psel.at[level], prec.at[level], sk_send.at[level], sk_recv.at[level], peer)
-    nb = [
-        send(pts_ref, nbp.at[0], nb_send.at[0], nb_recv.at[0], right),
-        send(pts_ref, nbp.at[1], nb_send.at[1], nb_recv.at[1], left),
-        send(r0_ref, nbr.at[0], nb_send.at[2], nb_recv.at[2], right),
-        send(r0_ref, nbr.at[1], nb_send.at[3], nb_recv.at[3], left),
-    ]
-    for level in order[2:]:
         send_coefs(level)
+        if i == min(1, levels - 1):
+            nb = [
+                send(pts_ref, nbp.at[0], nb_send.at[0], nb_recv.at[0], right),
+                send(pts_ref, nbp.at[1], nb_send.at[1], nb_recv.at[1], left),
+                send(r0_ref, nbr.at[0], nb_send.at[2], nb_recv.at[2], right),
+                send(r0_ref, nbr.at[1], nb_send.at[3], nb_recv.at[3], left),
+            ]
 
     acc_k[...] = jnp.zeros_like(acc_k)
     slope_ref[...] = jnp.zeros_like(slope_ref)
@@ -296,8 +294,6 @@
             chi[level] = hi
             clo[level] = low
 
-    couplings(arrivals[:4])
-
     valid = [jnp.where(me > 0, 1.0, 0.0), jnp.where(me < n - 1, 1.0, 0.0)]
     for side, slot in ((0, 0), (1, 2)):
         nb[side].wait_recv()
@@ -315,6 +311,7 @@
     rough = noise * r0 + sig * (near_now[0:16] + near_now[16:32] + near_now[32:33] * r0)
     first_a = start_reduce(0, pack([row_dot(r0, r0), row_dot(r0, rough)]))
 
+    couplings(arrivals[:4])
     couplings(arrivals[4:])
 
     def mix(copy, received, level, with_ones):

time: 59.2 us -> 59.1 us (level)
  no operation moved by 1% of the time
where the time goes in v6:
time: 59.1 us; the launch traced here: 58.9 us
  Pallas kernels  55.7 us (94%)
  between operations  3.22 us (5%)
    pallas_call x1, Pallas kernels, shards(): pl.pallas_call(functools.partial(kernel, bits, groups), out_shape=(block,...  54.9 us

profile of v6, /device:TPU:1, one launch (start us, length us, event | category | flops | bytes accessed | tf_op | source)
XLA Modules:
  0.0 58.9 jit_solution(843247410087970355)
XLA Ops:
  3.2 54.9 %cg.1 = (f32[16,1024]{1,0:T(8,128)S(1)}, f32[16,1024]{1,0:T(8,128)S(1)}, f32[16,1024]{1,0:T(8,128)S(1)}, f32[16,1024]{1,0:T(8,128)S(1)}, f32[1,128]{1,0:T(1,128)S(1)}, /*index=5*/f32[1,128]{1,0:T(1,128)S(1)}) custom-call(f32[3,1024]{1,0:T(4,128)} %pts_hbm.1, f32[16,1024]{1,0:T(8,128)} %r0_hbm.1, s32[8,256]{1,0:T(8,128)} %skel_hbm.1, f32[1]{0:T(128)S(6)} %copy.11.len_ref, ...), custom_call_target="tpu_custom_call" | custom-call | tf_op jit(solution)/shard_map/cg/pallas_call | solution.py:507
  58.1 0.8 %finish.1 = (f32[16,1024]{1,0:T(8,128)}, f32[16,1024]{1,0:T(8,128)}, f32[16,1024]{1,0:T(8,128)}, f32[1,16]{1,0:T(1,128)}) custom-call(f32[16,1024]{1,0:T(8,128)S(1)} %get-tuple-element.14.r1_ref, f32[16,1024]{1,0:T(8,128)S(1)} %get-tuple-element.15.r1_image_ref, f32[16,1024]{1,0:T(8,128)S(1)} %get-tuple-element.16.q_ref, ...), custom_call_target="tpu_custom_call" | custom-call | tf_op jit(solution)/shard_map/finish/pallas_call | solution.py:517
